TPU v7x, 256 devices: a whole 4x4x8 slice. The times are simulated.
256 devices in a mesh: dp: 16 (over y, z_lo), expert: 16 (over z_hi, x, core).
Axes of the slice: x: 4, y: 4, z: 8 (z_hi: 2, z_lo: 4; z = z_hi * 4 + z_lo), core: 2. Of those that a mesh axis runs over, the one named last changes fastest.
Arguments:
- tokens: bfloat16 [65536, 1024], P(('dp', 'expert')), may hold values from -6 to 6
- out_grad: bfloat16 [65536, 1024], P(('dp', 'expert')), may hold values from -3 to 3
- gate_prob: bfloat16 [65536], P(('dp', 'expert')), may hold values from 0.19921875 to 1
- expert_id: int32 [65536], P(('dp', 'expert')), may hold values from 0 to 15, as said below
- up_weight: bfloat16 [16, 1024, 2048], P('expert'), may hold values from -0.1875 to 0.1875
- down_weight: bfloat16 [16, 2048, 1024], P('expert'), may hold values from -0.125 to 0.125
Outputs:
- tokens_grad: bfloat16 [65536, 1024], P(('dp', 'expert'))
- gate_grad: bfloat16 [65536], P(('dp', 'expert'))
- up_weight_grad: float32 [16, 1024, 2048], P('expert', 'dp')
- down_weight_grad: float32 [16, 2048, 1024], P('expert', 'dp')
Inputs may be any that keep to these rules, and one draw needn't show every extreme that they name: `expert_id`: among the 256 tokens of one device each expert is named at most 32 times; in every data group one expert is named exactly 32 times by every device of the group.
All inputs are finite; a program needn't handle non-finite values.
Results may differ from a plain program's by a relative error of at most 0.017.
Values may be sent and summed in bfloat16 or wider, within the bound.
A program may use at most 64 MiB of HBM per device.

v0:
```python
import jax
import jax.numpy as jnp
from jax import lax
from jax.sharding import PartitionSpec as P

SQRT_HALF = 0.7071067811865476
INV_ROOT_TAU = 0.3989422804014327


def gelu_value(pre_act):
    return 0.5 * pre_act * (1.0 + jax.scipy.special.erf(pre_act * SQRT_HALF))


def gelu_slope(pre_act):
    normal_cdf = 0.5 * (1.0 + jax.scipy.special.erf(pre_act * SQRT_HALF))
    return normal_cdf + pre_act * jnp.exp(-0.5 * pre_act * pre_act) * INV_ROOT_TAU


def contract_rows(left, right):
    return lax.dot_general(
        left, right, (((0,), (0,)), ((), ())), preferred_element_type=jnp.float32
    )


def expert_rows(feat_rows, grad_rows, gate_rows, up_matrix, down_matrix):
    pre_act = jnp.dot(feat_rows, up_matrix, preferred_element_type=jnp.float32)
    hidden = gelu_value(pre_act).astype(jnp.bfloat16)
    expert_out = jnp.dot(hidden, down_matrix, preferred_element_type=jnp.float32)
    gate_grad = jnp.sum(grad_rows.astype(jnp.float32) * expert_out, axis=1).astype(jnp.bfloat16)
    scaled = (gate_rows.astype(jnp.float32)[:, None] * grad_rows.astype(jnp.float32)).astype(
        jnp.bfloat16
    )
    hidden_grad = lax.dot_general(
        scaled, down_matrix, (((1,), (1,)), ((), ())), preferred_element_type=jnp.float32
    )
    pre_grad = (hidden_grad * gelu_slope(pre_act)).astype(jnp.bfloat16)
    feat_grad = lax.dot_general(
        pre_grad, up_matrix, (((1,), (1,)), ((), ())), preferred_element_type=jnp.float32
    ).astype(jnp.bfloat16)
    return (feat_grad, gate_grad, hidden, scaled, pre_grad)


def per_device(tokens, out_grad, gate_prob, expert_id, up_weight, down_weight):
    up_matrix = up_weight[0]
    down_matrix = down_weight[0]
    feat_width = tokens.shape[1]
    local_count = tokens.shape[0]
    experts = lax.axis_size("expert") * up_weight.shape[0]
    capacity = 2 * local_count // experts
    one_hot = (expert_id[:, None] == jnp.arange(experts, dtype=jnp.int32)[None, :]).astype(
        jnp.int32
    )
    running = jnp.cumsum(one_hot, axis=0)
    position = jnp.sum((running - one_hot) * one_hot, axis=1)
    slot_index = expert_id * capacity + position
    token_of_slot = (
        jnp.full((experts * capacity,), local_count, jnp.int32)
        .at[slot_index]
        .set(jnp.arange(local_count, dtype=jnp.int32))
    )
    feat_slots = jnp.take(tokens, token_of_slot, axis=0, mode="fill", fill_value=0).reshape(
        experts, capacity, feat_width
    )
    grad_slots = jnp.take(out_grad, token_of_slot, axis=0, mode="fill", fill_value=0).reshape(
        experts, capacity, feat_width
    )
    gate_slots = jnp.take(gate_prob, token_of_slot, axis=0, mode="fill", fill_value=0).reshape(
        experts, capacity
    )
    feat_recv, grad_recv, gate_recv = (
        lax.all_to_all(feat_slots, "expert", split_axis=0, concat_axis=0, tiled=True),
        lax.all_to_all(grad_slots, "expert", split_axis=0, concat_axis=0, tiled=True),
        lax.all_to_all(gate_slots, "expert", split_axis=0, concat_axis=0, tiled=True),
    )
    sources = gate_recv.shape[0]
    feat_rows = feat_recv.reshape(-1, feat_width)
    feat_grad, gate_grad, hidden, scaled, pre_grad = expert_rows(
        feat_rows, grad_recv.reshape(-1, feat_width), gate_recv.reshape(-1), up_matrix, down_matrix
    )
    feat_back, gate_back = (
        lax.all_to_all(
            feat_grad.reshape(sources, capacity, feat_width),
            "expert",
            split_axis=0,
            concat_axis=0,
            tiled=True,
        ),
        lax.all_to_all(
            gate_grad.reshape(sources, capacity), "expert", split_axis=0, concat_axis=0, tiled=True
        ),
    )
    divisor = 1.0 / lax.axis_size("dp")
    up_sum, down_sum = (
        lax.psum_scatter(
            contract_rows(feat_rows, pre_grad).astype(jnp.bfloat16),
            "dp",
            scatter_dimension=0,
            tiled=True,
        ).astype(jnp.float32),
        lax.psum_scatter(
            contract_rows(hidden, scaled).astype(jnp.bfloat16),
            "dp",
            scatter_dimension=0,
            tiled=True,
        ).astype(jnp.float32),
    )
    tokens_grad = feat_back.reshape(experts * capacity, feat_width)[slot_index]
    gate_result = gate_back.reshape(experts * capacity)[slot_index]
    return (tokens_grad, gate_result, (up_sum * divisor)[None], (down_sum * divisor)[None])


def solution(mesh):
    return jax.shard_map(
        per_device,
        mesh=mesh,
        in_specs=(
            P(("dp", "expert"), None),
            P(("dp", "expert"), None),
            P(("dp", "expert")),
            P(("dp", "expert")),
            P("expert", None, None),
            P("expert", None, None),
        ),
        out_specs=(
            P(("dp", "expert"), None),
            P(("dp", "expert")),
            P("expert", "dp", None),
            P("expert", "dp", None),
        ),
        check_vma=False,
    )
```

profile of v0, /device:TPU:64, one launch (start us, length us, event | category | flops | bytes accessed | tf_op | source)
XLA Modules:
  0.0 347.2 jit_solution(7725972703466275295)
XLA Ops:
  7.2 0.0 copy-start
  7.2 0.7 fusion.27
  7.9 0.6 reduce-window.6
  8.5 0.2 slice_reduce_fusion
  8.7 0.8 fusion.26
  9.5 0.7 compare_select_fusion.1
  10.2 1.4 scatter_custom_fusion
  11.6 3.5 gather_fusion
  15.1 0.7 select_n.41
  15.8 9.2 %all-to-all-start = ((bf16[16,1,32]{2,1,0:T(2,128)(2,1)}), bf16[16,1,32]{2,1,0:T(2,128)(2,1)S(1)}, u32[]{:S(2)}, u32[]{:S(2)}) async-start(bf16[16,1,32]{2,1,0:T(2,128)(2,1)} %select_n.41), calls=%async_computation | async-start | bytes 16384 | tf_op jit(solution)/shard_map/all_to_all | solution.py:73
  25.0 0.0 copy-done
  25.0 0.0 copy-start.1
  25.0 2.1 gather_fusion.4
  27.1 0.0 copy-done.1
  27.1 2.1 gather_fusion.3
  29.2 1.5 broadcast_select_fusion.1
  30.7 4.2 %all-to-all-done = bf16[16,1,32]{2,1,0:T(2,128)(2,1)S(1)} async-done(((bf16[16,1,32]{2,1,0:T(2,128)(2,1)}), bf16[16,1,32]{2,1,0:T(2,128)(2,1)S(1)}, u32[]{:S(2)}, u32[]{:S(2)}) %all-to-all-start) | async-done | bytes 1056 | tf_op jit(solution)/shard_map/all_to_all | solution.py:73
  34.9 37.0 %all_to_all.27 = bf16[16,32,1024]{2,1,0:T(8,128)(2,1)S(1)} all-to-all(bf16[16,32,1024]{2,1,0:T(8,128)(2,1)} %bitcast.67), channel_id=1, replica_groups=mesh['dp'=16,'expert'=16] {'expert'}, dimensions={0} | all-to-all | bytes 2097152 | tf_op jit(solution)/shard_map/all_to_all | solution.py:71
  71.9 3.7 %all-to-all-start.1 = ((bf16[16,32,1024]{2,1,0:T(8,128)(2,1)}), bf16[16,32,1024]{2,1,0:T(8,128)(2,1)S(1)}, u32[]{:S(2)}, u32[]{:S(2)}) async-start(bf16[16,32,1024]{2,1,0:T(8,128)(2,1)} %bitcast.66), calls=%async_computation.1 | async-start | bytes 2097152 | tf_op jit(solution)/shard_map/all_to_all | solution.py:72
  75.6 0.0 reduce-scatter.3.cloned.1.call-start
  75.6 6.6 %multiply_convert_fusion = (bf16[512,2048]{1,0:T(8,128)(2,1)}, f32[512,2048]{1,0:T(8,128)}) fusion(bf16[512,1024]{1,0:T(8,128)(2,1)S(1)} %bitcast.68, bf16[1,1024,2048]{2,1,0:T(8,128)(2,1)} %param.12), kind=kOutput, calls=%fused_computation.21 | convolution fusion | flops 2152726528 | bytes 11534336 | tf_op jit(solution)/shard_map/dot_general | solution.py:26
  82.3 22.7 %all-to-all-done.1 = bf16[16,32,1024]{2,1,0:T(8,128)(2,1)S(1)} async-done(((bf16[16,32,1024]{2,1,0:T(8,128)(2,1)}), bf16[16,32,1024]{2,1,0:T(8,128)(2,1)S(1)}, u32[]{:S(2)}, u32[]{:S(2)}) %all-to-all-start.1) | async-done | bytes 1048608 | tf_op jit(solution)/shard_map/all_to_all | solution.py:72
  104.9 0.2 fusion.16
  105.2 6.3 %fusion.5 = bf16[512,2048]{1,0:T(8,128)(2,1)S(1)} fusion(f32[512,2048]{1,0:T(8,128)} %get-tuple-element.10, bf16[512,1024]{1,0:T(8,128)(2,1)S(1)} %bitcast.70, bf16[1,2048,1024]{2,1,0:T(8,128)(2,1)} %param.13), kind=kOutput, calls=%fused_computation.12 | convolution fusion | flops 2157969408 | bytes 11534336 | tf_op jit(solution)/shard_map/dot_general | solution.py:33
  111.5 0.0 copy-start.2
  111.5 1.3 copy-done.2
  112.8 4.3 %convolution_convert_fusion.1 = bf16[1024,2048]{1,0:T(8,128)(2,1)} fusion(bf16[512,1024]{1,0:T(8,128)(2,1)S(1)} %bitcast.69, bf16[512,2048]{1,0:T(8,128)(2,1)S(1)} %fusion.5), kind=kOutput, calls=%fused_computation.24 | convolution fusion | flops 2149580800 | bytes 7340032 | tf_op jit(solution)/shard_map/dot_general | solution.py:20
  117.1 0.0 reduce-scatter.3.cloned.1.call-update
  117.1 0.2 reduce-scatter.5.cloned.1.call-start
  117.4 0.1 reshape.122
  117.5 0.2 fusion.18
  117.7 5.9 %convolution_convert_fusion = bf16[2048,1024]{1,0:T(8,128)(2,1)} fusion(bf16[512,2048]{1,0:T(8,128)(2,1)} %get-tuple-element.9, bf16[512,1024]{1,0:T(8,128)(2,1)S(1)} %fusion.18), kind=kOutput, calls=%fused_computation.23 | convolution fusion | flops 2149580800 | bytes 7340032 | tf_op jit(solution)/shard_map/dot_general | solution.py:20
  123.7 0.0 reduce-scatter.5.cloned.1.call-update
  123.7 5.4 %fusion.17 = bf16[512]{0:T(512)(128)(2,1)S(1)} fusion(bf16[16,32,1024]{2,1,0:T(8,128)(2,1)S(1)} %all-to-all-done.1, bf16[512,2048]{1,0:T(8,128)(2,1)} %get-tuple-element.9, bf16[1,2048,1024]{2,1,0:T(8,128)(2,1)} %param.13), kind=kOutput, calls=%fused_computation.29 | convolution fusion | flops 2149056000 | bytes 7341056 | tf_op jit(solution)/shard_map/dot_general | solution.py:28
  129.1 0.7 convert_element_type.100
  129.8 3.5 all-to-all-start.4
  133.3 6.3 %fusion.21 = bf16[512,1024]{1,0:T(8,128)(2,1)} fusion(bf16[512,2048]{1,0:T(8,128)(2,1)} %copy-done.2, bf16[1,1024,2048]{2,1,0:T(8,128)(2,1)} %param.12), kind=kOutput, calls=%fused_computation.31 | convolution fusion | flops 2148007936 | bytes 7340032 | tf_op jit(solution)/shard_map/dot_general | solution.py:37
  139.6 3.6 %all-to-all-done.4 = bf16[16,1,32]{2,1,0:T(2,128)(2,1)S(1)} async-done(((bf16[16,1,32]{2,1,0:T(2,128)(2,1)}), bf16[16,1,32]{2,1,0:T(2,128)(2,1)S(1)}, u32[]{:S(2)}, u32[]{:S(2)}) %all-to-all-start.4) | async-done | bytes 1056 | tf_op jit(solution)/shard_map/all_to_all | solution.py:88
  143.2 6.0 %all-to-all-start.3 = ((bf16[16,32,1024]{2,1,0:T(8,128)(2,1)}), bf16[16,32,1024]{2,1,0:T(8,128)(2,1)S(1)}, u32[]{:S(2)}, u32[]{:S(2)}) async-start(bf16[16,32,1024]{2,1,0:T(8,128)(2,1)} %bitcast.9), calls=%async_computation.3 | async-start | bytes 2097152 | tf_op jit(solution)/shard_map/all_to_all | solution.py:81
  149.2 0.1 reshape.119
  149.3 2.4 gather_fusion.2
  151.7 51.2 %all-to-all-done.3 = bf16[16,32,1024]{2,1,0:T(8,128)(2,1)S(1)} async-done(((bf16[16,32,1024]{2,1,0:T(8,128)(2,1)}), bf16[16,32,1024]{2,1,0:T(8,128)(2,1)S(1)}, u32[]{:S(2)}, u32[]{:S(2)}) %all-to-all-start.3) | async-done | bytes 1048608 | tf_op jit(solution)/shard_map/all_to_all | solution.py:81
  203.0 2.0 gather_fusion.1
  204.9 30.4 %reduce-scatter.3.cloned.1.call-done = bf16[64,2048]{1,0:T(8,128)(2,1)} async-done(((bf16[1024,2048]{1,0:T(8,128)(2,1)}), bf16[64,2048]{1,0:T(8,128)(2,1)}) %reduce-scatter.3.cloned.1.call-update) | async-done | bytes 262160 | tf_op jit(solution)/shard_map/reduce_scatter | solution.py:94
  235.4 1.8 multiply_bitcast_fusion.1
  237.1 101.5 %reduce-scatter.5.cloned.1.call-done = bf16[128,1024]{1,0:T(8,128)(2,1)} async-done(((bf16[2048,1024]{1,0:T(8,128)(2,1)}), bf16[128,1024]{1,0:T(8,128)(2,1)}) %reduce-scatter.5.cloned.1.call-update) | async-done | bytes 262160 | tf_op jit(solution)/shard_map/reduce_scatter | solution.py:100
  338.6 1.8 multiply_bitcast_fusion
  (10 shorter events, 0.1 us)
Async XLA Ops:
  7.2 17.9 %copy-start = (bf16[256,1024]{1,0:T(8,128)(2,1)S(1)}, bf16[256,1024]{1,0:T(8,128)(2,1)}, u32[]{:S(2)}) copy-start(bf16[256,1024]{1,0:T(8,128)(2,1)} %param.8) | copy-start | bytes 1572868
  15.8 19.2 %all-to-all-start = ((bf16[16,1,32]{2,1,0:T(2,128)(2,1)}), bf16[16,1,32]{2,1,0:T(2,128)(2,1)S(1)}, u32[]{:S(2)}, u32[]{:S(2)}) async-start(bf16[16,1,32]{2,1,0:T(2,128)(2,1)} %select_n.41), calls=%async_computation | async-start | bytes 16384 | tf_op jit(solution)/shard_map/all_to_all | solution.py:73
  25.0 2.1 copy-start.1
  71.9 33.0 %all-to-all-start.1 = ((bf16[16,32,1024]{2,1,0:T(8,128)(2,1)}), bf16[16,32,1024]{2,1,0:T(8,128)(2,1)S(1)}, u32[]{:S(2)}, u32[]{:S(2)}) async-start(bf16[16,32,1024]{2,1,0:T(8,128)(2,1)} %bitcast.66), calls=%async_computation.1 | async-start | bytes 2097152 | tf_op jit(solution)/shard_map/all_to_all | solution.py:72
  75.6 159.8 %reduce-scatter.3.cloned.1.call-start = ((), (), s32[]{:S(2)}) async-start(), calls=%async_computation.7 | async-start | bytes 4456448 | tf_op jit(solution)/shard_map/reduce_scatter | solution.py:94
  111.5 1.3 copy-start.2
  117.1 221.5 %reduce-scatter.5.cloned.1.call-start = ((), (), s32[]{:S(2)}) async-start(), calls=%async_computation.8 | async-start | bytes 4456448 | tf_op jit(solution)/shard_map/reduce_scatter | solution.py:100
  129.8 13.3 %all-to-all-start.4 = ((bf16[16,1,32]{2,1,0:T(2,128)(2,1)}), bf16[16,1,32]{2,1,0:T(2,128)(2,1)S(1)}, u32[]{:S(2)}, u32[]{:S(2)}) async-start(bf16[16,1,32]{2,1,0:T(2,128)(2,1)} %convert_element_type.100), calls=%async_computation.4 | async-start | bytes 16384 | tf_op jit(solution)/shard_map/all_to_all | solution.py:88
  143.2 59.8 %all-to-all-start.3 = ((bf16[16,32,1024]{2,1,0:T(8,128)(2,1)}), bf16[16,32,1024]{2,1,0:T(8,128)(2,1)S(1)}, u32[]{:S(2)}, u32[]{:S(2)}) async-start(bf16[16,32,1024]{2,1,0:T(8,128)(2,1)} %bitcast.9), calls=%async_computation.3 | async-start | bytes 2097152 | tf_op jit(solution)/shard_map/all_to_all | solution.py:81
Sparse Core Ops, SparseCore 0:
  117.3 118.0 reduce-scatter.2
  237.9 100.6 reduce-scatter.4
where the time goes:
time: 354 us; the launch traced here: 347 us
  waiting for transfers between devices  214 us (60%)
  blocking collectives  37 us (10%)
  matrix products  34.9 us (10%)
  starting transfers between devices  22.6 us (6%)
  local copies, waits for them, and re-layouts  16.4 us (5%)
  between operations  14.2 us (4%)
  other arithmetic  8.47 us (2%)
    reduce_scatter x1, waiting for transfers between devices, per_device(): lax.psum_scatter(contract_rows(hidden, scaled).astype(jnp.bfloat16), 'dp'...  101 us
    all_to_all x1, waiting for transfers between devices, per_device(): lax.all_to_all(feat_grad.reshape(sources, capacity, feat_width), 'expert'...  51.2 us
    all_to_all x1, blocking collectives, per_device(): lax.all_to_all(feat_slots, 'expert', split_axis=0, concat_axis=0, tiled=T...  37 us
    reduce_scatter x1, waiting for transfers between devices, per_device(): lax.psum_scatter(contract_rows(feat_rows, pre_grad).astype(jnp.bfloat16),...  30.4 us
    all_to_all x1, waiting for transfers between devices, per_device(): lax.all_to_all(grad_slots, 'expert', split_axis=0, concat_axis=0, tiled=T...  22.7 us
    dot_general x2, matrix products, contract_rows(): lax.dot_general(left, right, (((0,), (0,)), ((), ())), preferred_element_...  10.3 us
    all_to_all x1, starting transfers between devices, per_device(): lax.all_to_all(gate_slots, 'expert', split_axis=0, concat_axis=0, tiled=T...  9.23 us
  transfers between devices with their start and end apart: 6, of which 6 were waited for; matrix products, arithmetic and copies ran while one was open for 11% of the time, Pallas kernels for 0%

commit v1 on v0

v1 whole, which is shorter than its diff:
```python
import jax
import jax.numpy as jnp
from jax import lax
from jax.experimental import pallas as pl
from jax.experimental.pallas import tpu as pltpu
from jax.sharding import PartitionSpec as P

MESH = pl.DeviceIdType.MESH
SQRT_HALF = 0.7071067811865476
INV_ROOT_TAU = 0.3989422804014327
BF = jnp.bfloat16
F32 = jnp.float32
D = 1024
FF = 2048
TOK = 256
CAP = 32
NY = 4
NZ = 4
LANES = 128


def dot(a, b, ca, cb):
    return lax.dot_general(a, b, (((ca,), (cb,)), ((), ())), preferred_element_type=F32)


def iota(shape, axis):
    return lax.broadcasted_iota(jnp.int32, shape, axis)


def to_column(row):
    n = row.shape[1]
    eye = iota((n, n), 0) == iota((n, n), 1)
    return jnp.sum(jnp.where(eye, row, 0.0), axis=1, keepdims=True)


def kernel(
    tok_hbm, og_hbm, gate_ref, id_ref, upw_hbm, dnw_hbm,
    tg_ref, gg_ref, ug_ref, dg_ref,
    tok, og, upw, dnw, slots, recv, hidden, pregrad, fgs, back, ggs, ggback,
    s1u, s1d, ou, od, du, dd, r1u, r1d, rou, rod, rdu, rdd,
    zu, zd, zlu, zld, zru, zrd, fu, fd, pu, su, sd,
    in_sem, ds_sem, dr_sem, bs_sem, br_sem, gs_sem, gr_sem, ys_sem, yr_sem, zs_sem, zl_sem, zr_sem,
):
    dp = lax.axis_index("dp")
    ex = lax.axis_index("expert")
    y, zl = dp // NZ, dp % NZ
    zh, j = ex // 8, ex % 8

    def group_dp(h):
        return y * NZ + (NZ - 1 - zl) if h else dp

    def group_ex(h, other):
        return ((1 - zh) if h else zh) * 8 + other

    def dest(h, i):
        return (group_dp(h), group_ex(h, (j + i) % 8))

    def source(h, i):
        return (group_dp(h), group_ex(h, (j + 8 - i) % 8))

    plus = (((y + 1) % NY) * NZ + zl, ex)
    minus = (((y + NY - 1) % NY) * NZ + zl, ex)
    right = (dp + 1, ex)
    left = (dp - 1, ex)
    pairs = [(h, i) for h in (1, 0) for i in range(8) if (h, i) != (0, 0)]

    loads = [
        pltpu.make_async_copy(src, dst, in_sem.at[n])
        for n, (src, dst) in enumerate(
            ((tok_hbm, tok), (og_hbm, og), (upw_hbm, upw), (dnw_hbm, dnw))
        )
    ]
    for load in loads:
        load.start()

    barrier = pltpu.get_barrier_semaphore()
    for h, i in pairs:
        pl.semaphore_signal(barrier, inc=1, device_id=dest(h, i), device_id_type=MESH)
    for who in (plus, minus):
        pl.semaphore_signal(barrier, inc=1, device_id=who, device_id_type=MESH)

    @pl.when(zl < NZ - 1)
    def _():
        pl.semaphore_signal(barrier, inc=1, device_id=right, device_id_type=MESH)

    @pl.when(zl > 0)
    def _():
        pl.semaphore_signal(barrier, inc=1, device_id=left, device_id_type=MESH)

    ids = id_ref[...]
    ids_row = ids.astype(F32)
    ids_col = to_column(ids_row)
    same = ids_col == ids_row
    before = iota((TOK, TOK), 0) < iota((TOK, TOK), 1)
    after = iota((TOK, TOK), 1) < iota((TOK, TOK), 0)
    pos_row = jnp.sum(jnp.where(same & before, 1.0, 0.0), axis=0, keepdims=True)
    pos_col = jnp.sum(jnp.where(same & after, 1.0, 0.0), axis=1, keepdims=True)

    def slot_of(ident, place):
        mine = zh.astype(F32)
        half = jnp.where(ident >= 8.0, 1.0, 0.0)
        rank = ident - 8.0 * half - j.astype(F32)
        rank = jnp.where(rank < 0.0, rank + 8.0, rank)
        cross = jnp.abs(half - mine)
        return cross * 256.0 + rank * 32.0 + place

    slot_row = slot_of(ids_row, pos_row)
    slot_col = slot_of(ids_col, pos_col)
    gate_row = gate_ref[...].astype(F32)
    gate_col = to_column(gate_row)

    loads[0].wait()
    loads[1].wait()
    og[...] = (gate_col * og[...].astype(F32)).astype(BF)

    pl.semaphore_wait(barrier, 17 + (zl < NZ - 1).astype(jnp.int32) + (zl > 0).astype(jnp.int32))

    def dispatch(h, i):
        return pltpu.make_async_remote_copy(
            src_ref=slots.at[h, i], dst_ref=recv.at[h, i],
            send_sem=ds_sem.at[h, i], recv_sem=dr_sem.at[h, i],
            device_id=dest(h, i), device_id_type=MESH,
        )

    for h in (1, 0):
        place = (iota((TOK, TOK), 0) + TOK * h).astype(F32)
        pick = jnp.where(place == slot_row, 1.0, 0.0).astype(BF)
        slots[h, :, :CAP, :] = dot(pick, tok[...], 1, 0).astype(BF).reshape(8, CAP, D)
        slots[h, :, CAP:, :] = dot(pick, og[...], 1, 0).astype(BF).reshape(8, CAP, D)
        for i in range(8):
            if (h, i) != (0, 0):
                dispatch(h, i).start()
    recv[0, 0] = slots[0, 0]
    loads[2].wait()
    loads[3].wait()

    def rows_of(h, q):
        return pl.ds((h * 2 + q) * LANES, LANES)

    def forward(h, q):
        rows = rows_of(h, q)
        for i in range(4 * q, 4 * q + 4):
            if (h, i) != (0, 0):
                dispatch(h, i).wait_recv()

        def body(n, acc):
            cols = pl.ds(pl.multiple_of(n * 512, 512), 512)
            feat = recv[h, 4 * q : 4 * q + 4, :CAP, :].reshape(LANES, D)
            scaled = recv[h, 4 * q : 4 * q + 4, CAP:, :].reshape(LANES, D)
            pre = dot(feat, upw[:, cols], 1, 0)
            hgrad = dot(scaled, dnw[cols, :], 1, 1)
            cdf = 0.5 * (1.0 + lax.erf(pre * SQRT_HALF))
            hid = (pre * cdf).astype(BF)
            slope = cdf + pre * jnp.exp(-0.5 * pre * pre) * INV_ROOT_TAU
            hidden[rows, cols] = hid
            pregrad[rows, cols] = (hgrad * slope).astype(BF)
            return acc + jnp.sum(hid.astype(F32) * hgrad, axis=1, keepdims=True)

        total = lax.fori_loop(0, FF // 512, body, jnp.zeros((LANES, 1), F32))
        eye = iota((CAP, LANES), 0) == iota((CAP, LANES), 1)
        for i in range(4):
            part = total[i * CAP : (i + 1) * CAP, :]
            row = jnp.sum(jnp.where(eye, part, 0.0), axis=0, keepdims=True)
            ggs[h, 4 * q + i] = jnp.broadcast_to(row, (8, LANES))

    def give_back(h, i):
        return pltpu.make_async_remote_copy(
            src_ref=fgs.at[h, i], dst_ref=back.at[h, i],
            send_sem=bs_sem.at[h, i], recv_sem=br_sem.at[h, i],
            device_id=source(h, i), device_id_type=MESH,
        )

    def give_gate(h, i):
        return pltpu.make_async_remote_copy(
            src_ref=ggs.at[h, i], dst_ref=ggback.at[h, i],
            send_sem=gs_sem.at[h, i], recv_sem=gr_sem.at[h, i],
            device_id=source(h, i), device_id_type=MESH,
        )

    def feature_grad(h, q):
        rows = rows_of(h, q)

        @pl.loop(0, D // 512)
        def _(n):
            cols = pl.ds(pl.multiple_of(n * 512, 512), 512)
            fg = dot(pregrad[rows, :], upw[cols, :], 1, 1).astype(BF)
            fgs[h, 4 * q : 4 * q + 4, :, cols] = fg.reshape(4, CAP, 512)

        for i in range(4 * q, 4 * q + 4):
            if (h, i) == (0, 0):
                back[0, 0] = fgs[0, 0]
                ggback[0, 0] = ggs[0, 0]
            else:
                give_back(h, i).start()
                give_gate(h, i).start()

    forward(0, 0)
    forward(0, 1)
    feature_grad(0, 0)
    feature_grad(0, 1)
    forward(1, 0)
    forward(1, 1)

    def up_pair(chunk, m, emit):
        @pl.loop(0, FF // 512)
        def _(n):
            cols = pl.ds(pl.multiple_of(n * 512, 512), 512)
            feats = pl.ds(pl.multiple_of(chunk * 256 + m * LANES, LANES), LANES)
            lhs = recv[:, :, :CAP, feats].reshape(512, LANES)
            emit(cols, dot(lhs, pregrad[:, cols], 0, 0))

    def down_block(chunk, k, emit):
        @pl.loop(0, D // 512)
        def _(n):
            cols = pl.ds(pl.multiple_of(n * 512, 512), 512)
            feats = pl.ds(pl.multiple_of(chunk * 512 + k * LANES, LANES), LANES)
            rhs = recv[:, :, CAP:, cols].reshape(512, 512)
            emit(cols, dot(hidden[:, feats], rhs, 0, 0))

    yrefs = (
        (s1u, r1u, plus), (s1d, r1d, minus), (ou, rou, minus),
        (od, rod, plus), (du, rdu, plus), (dd, rdd, minus),
    )

    def ysend(which, k):
        src, dst, who = yrefs[which]
        return pltpu.make_async_remote_copy(
            src_ref=src.at[k], dst_ref=dst.at[k],
            send_sem=ys_sem.at[which, k], recv_sem=yr_sem.at[which, k],
            device_id=who, device_id_type=MESH,
        )

    S1U, S1D, OU, OD, DU, DD = range(6)
    far, nxt, prv = (y + 2) % NY, (y + 1) % NY, (y + NY - 1) % NY

    def order(m, s):
        return 2 * m + (s + m) % 2

    def store_pair(ref, m):
        def emit(cols, v):
            ref[2 * m, :, cols] = v[:64].astype(BF)
            ref[2 * m + 1, :, cols] = v[64:].astype(BF)

        return emit

    def add_pair(ref, other, m):
        def emit(cols, v):
            ref[2 * m, :, cols] = (v[:64] + other[2 * m, :, cols].astype(F32)).astype(BF)
            ref[2 * m + 1, :, cols] = (v[64:] + other[2 * m + 1, :, cols].astype(F32)).astype(BF)

        return emit

    def store_block(ref, k):
        def emit(cols, v):
            ref[k, :, cols] = v.astype(BF)

        return emit

    def add_block(ref, other, k):
        def emit(cols, v):
            ref[k, :, cols] = (v + other[k, :, cols].astype(F32)).astype(BF)

        return emit

    @pl.loop(0, 2)
    def _(m):
        up_pair(far, m, store_pair(s1u, m))
        for s in range(2):
            k = order(m, s)
            ysend(S1U, k).start()
            down_block(far, k, store_block(s1d, k))
            ysend(S1D, k).start()

    feature_grad(1, 0)
    feature_grad(1, 1)

    @pl.loop(0, 2)
    def _(m):
        up_pair(prv, m, store_pair(ou, m))
        for s in range(2):
            ysend(S1U, order(m, s)).wait_recv()
        up_pair(nxt, m, add_pair(du, r1u, m))
        for s in range(2):
            k = order(m, s)
            ysend(OU, k).start()
            down_block(nxt, k, store_block(od, k))
            ysend(OD, k).start()
            ysend(DU, k).start()
            ysend(S1D, k).wait_recv()
            down_block(prv, k, add_block(dd, r1d, k))
            ysend(DD, k).start()

    for h, i in pairs:
        give_back(h, i).wait_recv()
        give_gate(h, i).wait_recv()
    spread = jnp.where(iota((TOK, 512), 1).astype(F32) == slot_col, 1.0, 0.0).astype(BF)

    @pl.loop(0, D // 512)
    def _(n):
        cols = pl.ds(pl.multiple_of(n * 512, 512), 512)
        rows = back[:, :, :, cols].reshape(512, 512)
        tg_ref[:, cols] = dot(spread, rows, 1, 0).astype(BF)

    lane = iota((TOK, LANES), 1).astype(F32)
    gate_sum = jnp.zeros((TOK, LANES), F32)
    for h in range(2):
        for i in range(8):
            base = float(h * 256 + i * CAP)
            hit = (lane < float(CAP)) & (lane + base == slot_col)
            gate_sum += jnp.where(hit, ggback[h, i, 0:1, :], 0.0)
    gate_total = jnp.sum(gate_sum, axis=1, keepdims=True) / gate_col
    eye = iota((TOK, TOK), 0) == iota((TOK, TOK), 1)
    gg_ref[...] = jnp.sum(jnp.where(eye, gate_total, 0.0), axis=0, keepdims=True).astype(BF)

    zrefs = ((zu, zlu, zru), (zd, zld, zrd))

    def zright(t, k):
        src, dst, _ = zrefs[t]
        return pltpu.make_async_remote_copy(
            src_ref=src.at[k], dst_ref=dst.at[k],
            send_sem=zs_sem.at[t, k], recv_sem=zl_sem.at[t, k],
            device_id=right, device_id_type=MESH,
        )

    def zleft(t, k):
        src, _, dst = zrefs[t]
        return pltpu.make_async_remote_copy(
            src_ref=src.at[k], dst_ref=dst.at[k],
            send_sem=zs_sem.at[t, k], recv_sem=zr_sem.at[t, k],
            device_id=left, device_id_type=MESH,
        )

    def line(t, k, total, final):
        out, from_left, from_right = zrefs[t]

        @pl.when(zl == k)
        def _():
            final[...] = total[...]

        @pl.when((zl < k) & (zl == 0))
        def _():
            out[k] = total[...].astype(BF)

        @pl.when((zl < k) & (zl > 0))
        def _():
            zright(t, k).wait_recv()
            out[k] = (total[...] + from_left[k].astype(F32)).astype(BF)

        @pl.when(zl < k)
        def _():
            zright(t, k).start()

        @pl.when((zl > k) & (zl == NZ - 1))
        def _():
            out[k] = total[...].astype(BF)

        @pl.when((zl > k) & (zl < NZ - 1))
        def _():
            zleft(t, k).wait_recv()
            out[k] = (total[...] + from_right[k].astype(F32)).astype(BF)

        @pl.when(zl > k)
        def _():
            zleft(t, k).start()

    @pl.loop(0, 2)
    def _(m):
        def emit_pu(cols, v):
            pu[0, :, cols] = v[:64]
            pu[1, :, cols] = v[64:]

        up_pair(y, m, emit_pu)
        for s in range(2):
            k = order(m, s)

            def emit_sd(cols, v):
                sd[:, cols] = v

            down_block(y, k, emit_sd)
            ysend(DU, k).wait_recv()
            ysend(OU, k).wait_recv()
            su[...] = pu[(s + m) % 2] + rdu[k].astype(F32) + rou[k].astype(F32)
            line(0, k, su, fu)
            ysend(OD, k).wait_recv()
            ysend(DD, k).wait_recv()
            sd[...] = sd[...] + rod[k].astype(F32) + rdd[k].astype(F32)
            line(1, k, sd, fd)

    for t, final in ((0, fu), (1, fd)):
        _, from_left, from_right = zrefs[t]

        @pl.when(zl > 0)
        def _():
            zright(t, zl).wait_recv()
            final[...] = final[...] + from_left[zl].astype(F32)

        @pl.when(zl < NZ - 1)
        def _():
            zleft(t, zl).wait_recv()
            final[...] = final[...] + from_right[zl].astype(F32)

    scale = 1.0 / (NY * NZ)
    ug_ref[...] = fu[...] * scale
    dg_ref[...] = fd[...] * scale

    for h, i in pairs:
        dispatch(h, i).wait_send()
        give_back(h, i).wait_send()
        give_gate(h, i).wait_send()

    @pl.loop(0, 4)
    def _(k):
        for which in range(6):
            ysend(which, k).wait_send()

        @pl.when(zl != k)
        def _():
            zright(0, k).wait_send()
            zright(1, k).wait_send()


def per_device(tokens, out_grad, gate_prob, expert_id, up_weight, down_weight):
    any_spec = pl.BlockSpec(memory_space=pl.ANY)
    vmem = pl.BlockSpec(memory_space=pltpu.VMEM)
    up_blocks = pltpu.VMEM((4, 64, FF), BF)
    down_blocks = pltpu.VMEM((4, 128, D), BF)
    dma = pltpu.SemaphoreType.DMA
    tg, gg, ug, dg = pl.pallas_call(
        kernel,
        out_shape=(
            jax.ShapeDtypeStruct((TOK, D), BF),
            jax.ShapeDtypeStruct((1, TOK), BF),
            jax.ShapeDtypeStruct((64, FF), F32),
            jax.ShapeDtypeStruct((128, D), F32),
        ),
        in_specs=[any_spec, any_spec, vmem, vmem, any_spec, any_spec],
        out_specs=(vmem, vmem, vmem, vmem),
        scratch_shapes=[
            pltpu.VMEM((TOK, D), BF),
            pltpu.VMEM((TOK, D), BF),
            pltpu.VMEM((D, FF), BF),
            pltpu.VMEM((FF, D), BF),
            pltpu.VMEM((2, 8, 2 * CAP, D), BF),
            pltpu.VMEM((2, 8, 2 * CAP, D), BF),
            pltpu.VMEM((512, FF), BF),
            pltpu.VMEM((512, FF), BF),
            pltpu.VMEM((2, 8, CAP, D), BF),
            pltpu.VMEM((2, 8, CAP, D), BF),
            pltpu.VMEM((2, 8, 8, LANES), F32),
            pltpu.VMEM((2, 8, 8, LANES), F32),
            up_blocks, down_blocks, up_blocks, down_blocks, up_blocks, down_blocks,
            up_blocks, down_blocks, up_blocks, down_blocks, up_blocks, down_blocks,
            up_blocks, down_blocks, up_blocks, down_blocks, up_blocks, down_blocks,
            pltpu.VMEM((64, FF), F32),
            pltpu.VMEM((128, D), F32),
            pltpu.VMEM((2, 64, FF), F32),
            pltpu.VMEM((64, FF), F32),
            pltpu.VMEM((128, D), F32),
            dma((4,)),
            dma((2, 8)), dma((2, 8)), dma((2, 8)), dma((2, 8)), dma((2, 8)), dma((2, 8)),
            dma((6, 4)), dma((6, 4)), dma((2, 4)), dma((2, 4)), dma((2, 4)),
        ],
        compiler_params=pltpu.CompilerParams(
            collective_id=0, has_side_effects=True, vmem_limit_bytes=60 * 1024 * 1024
        ),
    )(
        tokens,
        out_grad,
        gate_prob.reshape(1, TOK),
        expert_id.reshape(1, TOK),
        up_weight[0],
        down_weight[0],
    )
    return tg, gg.reshape(TOK), ug[None], dg[None]


def solution(mesh):
    return jax.shard_map(
        per_device,
        mesh=mesh,
        in_specs=(
            P(("dp", "expert"), None),
            P(("dp", "expert"), None),
            P(("dp", "expert")),
            P(("dp", "expert")),
            P("expert", None, None),
            P("expert", None, None),
        ),
        out_specs=(
            P(("dp", "expert"), None),
            P(("dp", "expert")),
            P("expert", "dp", None),
            P("expert", "dp", None),
        ),
        check_vma=False,
    )
```

time: 354 us -> 173 us (0.49); the launches traced: 347 us -> 173 us
  waiting for transfers between devices: 214 us -> 0 us
  Pallas kernels: 0 us -> 164 us
  blocking collectives: 37 us -> 0 us
  matrix products: 34.9 us -> 0 us
  starting transfers between devices: 22.6 us -> 0 us
  between operations: 14.2 us -> 0.64 us
  local copies, waits for them, and re-layouts: 16.4 us -> 6.84 us
  other arithmetic: 8.47 us -> 1.19 us
    pallas_call x0 -> x1, Pallas kernels: none -> 164 us  [per_device(): pl.pallas_call(kernel, out_shape=(jax.ShapeDtypeStruct((TOK, D), BF), jax...]
    reduce_scatter x2 -> x0, waiting for transfers between devices: 132 us -> none  [the longest x1 101 us: per_device(): lax.psum_scatter(contract_rows(hidden, scaled).astype(jnp.bfloat16), 'dp'...]
    all_to_all x4 -> x0, waiting for transfers between devices: 81.7 us -> none  [the longest x1 51.2 us: per_device(): lax.all_to_all(feat_grad.reshape(sources, capacity, feat_width), 'expert'...]
    all_to_all x1 -> x0, blocking collectives: 37 us -> none  [per_device(): lax.all_to_all(feat_slots, 'expert', split_axis=0, concat_axis=0, tiled=T...]
    dot_general x6 -> x0, matrix products: 34.9 us -> none  [the longest x2 10.3 us: contract_rows(): lax.dot_general(left, right, (((0,), (0,)), ((), ())), preferred_element_...]
    all_to_all x4 -> x0, starting transfers between devices: 22.3 us -> none  [the longest x1 9.23 us: per_device(): lax.all_to_all(gate_slots, 'expert', split_axis=0, concat_axis=0, tiled=T...]
    gather x5 -> x0, local copies, waits for them, and re-layouts: 12 us -> none  [the longest x1 3.47 us: per_device(): jnp.take(gate_prob, token_of_slot, axis=0, mode='fill', fill_value=0)]
    unnamed x6 -> x3, local copies, waits for them, and re-layouts: 1.3 us -> 5.62 us
  transfers between devices with their start and end apart: 6 -> 0, of which waited for: 6 -> 0; matrix products, arithmetic and copies ran while one was open for 11% -> 0% of each run, Pallas kernels for 0% -> 0%
where the time goes in v1:
time: 173 us
  Pallas kernels  164 us (95%)
  local copies, waits for them, and re-layouts  6.84 us (4%)
    pallas_call x1, Pallas kernels, per_device(): pl.pallas_call(kernel, out_shape=(jax.ShapeDtypeStruct((TOK, D), BF), jax...  164 us
    unnamed x3, local copies, waits for them, and re-layouts  5.62 us

profile of v1, /device:TPU:64, one launch (start us, length us, event | category | flops | bytes accessed | tf_op | source)
XLA Modules:
  0.0 172.7 jit_solution(16527092538548212834)
XLA Ops:
  0.6 1.2 reshape.17.gate_ref
  1.9 164.1 %shard_map.93 = (bf16[256,1024]{1,0:T(8,128)(2,1)}, bf16[1,256]{1,0:T(2,128)(2,1)}, f32[64,2048]{1,0:T(8,128)}, f32[128,1024]{1,0:T(8,128)}) custom-call(bf16[256,1024]{1,0:T(8,128)(2,1)} %tok_hbm.1, bf16[256,1024]{1,0:T(8,128)(2,1)} %og_hbm.1, bf16[1,256]{1,0:T(2,128)(2,1)} %reshape.17.gate_ref, s32[1,256]{1,0:T(1,128)} %bitcast.9, ...), custom_call_target="tpu_custom_call" | custom-call | tf_op jit(solution)/shard_map/pallas_call | solution.py:428
  165.9 1.2 reduce
  167.1 1.9 %copy.13 = bf16[256,1024]{1,0:T(8,128)(2,1)} copy(bf16[256,1024]{1,0:T(8,128)(2,1)} %get-tuple-element.16) | data formatting | bytes 1048576
  169.0 1.9 %copy.14 = f32[1,64,2048]{2,1,0:T(8,128)} copy(f32[1,64,2048]{2,1,0:T(8,128)} %bitcast.8) | data formatting | bytes 1048576
  170.8 1.9 %copy.15 = f32[1,128,1024]{2,1,0:T(8,128)} copy(f32[1,128,1024]{2,1,0:T(8,128)} %bitcast.7) | data formatting | bytes 1048576

commit v2 on v1

v2 whole, which is shorter than its diff:
```python
import jax
import jax.numpy as jnp
from jax import lax
from jax.experimental import pallas as pl
from jax.experimental.pallas import tpu as pltpu
from jax.sharding import PartitionSpec as P

MESH = pl.DeviceIdType.MESH
SQRT_HALF = 0.7071067811865476
INV_ROOT_TAU = 0.3989422804014327
BF = jnp.bfloat16
F32 = jnp.float32
D = 1024
FF = 2048
TOK = 256
CAP = 32
NY = 4
NZ = 4
LANES = 128


def dot(a, b, ca, cb):
    return lax.dot_general(a, b, (((ca,), (cb,)), ((), ())), preferred_element_type=F32)


def iota(shape, axis):
    return lax.broadcasted_iota(jnp.int32, shape, axis)


def to_column(row):
    n = row.shape[1]
    eye = iota((n, n), 0) == iota((n, n), 1)
    return jnp.sum(jnp.where(eye, row, 0.0), axis=1, keepdims=True)


def kernel(
    tok_hbm, og_hbm, gate_ref, id_ref, upw_hbm, dnw_hbm,
    tg_ref, gg_ref, ug_ref, dg_ref,
    tok, og, upw, dnw, slots, rows, hidden, pregrad, fgp, fgr, fgs, back,
    gown, gp, gr, ggs, ggback,
    su_out, sd_out, su_in, sd_in, zu, zd, zlu, zld, zru, zrd, fu, fd, xu, pu, su, sd,
    in_sem, ds_sem, dr_sem, as_sem, ar_sem, fs_sem, fr_sem, hs_sem, hr_sem,
    bs_sem, br_sem, gs_sem, gr_sem, ys_sem, yr_sem, zs_sem, zl_sem, zr_sem, xs_sem, xr_sem,
):
    dp = lax.axis_index("dp")
    ex = lax.axis_index("expert")
    y, zl = dp // NZ, dp % NZ
    zh, j = ex // 8, ex % 8
    core = ex % 2
    near = y + 1 - 2 * (y % 2)
    flip = NY - 1 - y
    yr = near + core * (flip - near)
    yf = flip + core * (near - flip)
    yd = (y + 2) % NY

    def group_dp(h):
        return y * NZ + (NZ - 1 - zl) if h else dp

    def group_ex(h, other):
        return ((1 - zh) if h else zh) * 8 + other

    def dest(h, i):
        return (group_dp(h), group_ex(h, (j + i) % 8))

    def source(h, i):
        return (group_dp(h), group_ex(h, (j + 8 - i) % 8))

    mate = (yr * NZ + zl, ex)
    twin = (yf * NZ + zl, ex)
    right = (dp + 1, ex)
    left = (dp - 1, ex)
    pairs = [(h, i) for h in (1, 0) for i in range(8) if (h, i) != (0, 0)]

    sources = [
        (tok_hbm, tok),
        (og_hbm, og),
        (upw_hbm.at[:, pl.ds(pl.multiple_of(y * 512, 512), 512)], upw.at[:, 0:512]),
        (upw_hbm.at[:, pl.ds(pl.multiple_of(yf * 512, 512), 512)], upw.at[:, 512:1024]),
        (dnw_hbm.at[pl.ds(pl.multiple_of(y * 512, 512), 512), :], dnw.at[0:512, :]),
        (dnw_hbm.at[pl.ds(pl.multiple_of(yf * 512, 512), 512), :], dnw.at[512:1024, :]),
    ]
    loads = [
        pltpu.make_async_copy(src, dst, in_sem.at[n]) for n, (src, dst) in enumerate(sources)
    ]
    for load in loads:
        load.start()

    barrier = pltpu.get_barrier_semaphore()
    for h, i in pairs:
        pl.semaphore_signal(barrier, inc=1, device_id=dest(h, i), device_id_type=MESH)
    for who in (mate, twin):
        pl.semaphore_signal(barrier, inc=1, device_id=who, device_id_type=MESH)

    @pl.when(zl < NZ - 1)
    def _():
        pl.semaphore_signal(barrier, inc=1, device_id=right, device_id_type=MESH)

    @pl.when(zl > 0)
    def _():
        pl.semaphore_signal(barrier, inc=1, device_id=left, device_id_type=MESH)

    ids = id_ref[...]
    ids_row = ids.astype(F32)
    ids_col = to_column(ids_row)
    same = ids_col == ids_row
    before = iota((TOK, TOK), 0) < iota((TOK, TOK), 1)
    after = iota((TOK, TOK), 1) < iota((TOK, TOK), 0)
    pos_row = jnp.sum(jnp.where(same & before, 1.0, 0.0), axis=0, keepdims=True)
    pos_col = jnp.sum(jnp.where(same & after, 1.0, 0.0), axis=1, keepdims=True)

    def slot_of(ident, place):
        mine = zh.astype(F32)
        half = jnp.where(ident >= 8.0, 1.0, 0.0)
        rank = ident - 8.0 * half - j.astype(F32)
        rank = jnp.where(rank < 0.0, rank + 8.0, rank)
        cross = jnp.abs(half - mine)
        return cross * 256.0 + rank * 32.0 + place

    slot_row = slot_of(ids_row, pos_row)
    slot_col = slot_of(ids_col, pos_col)
    gate_row = gate_ref[...].astype(F32)
    gate_col = to_column(gate_row)

    loads[0].wait()
    loads[1].wait()
    og[...] = (gate_col * og[...].astype(F32)).astype(BF)

    pl.semaphore_wait(barrier, 17 + (zl < NZ - 1).astype(jnp.int32) + (zl > 0).astype(jnp.int32))

    def dispatch(h, i):
        return pltpu.make_async_remote_copy(
            src_ref=slots.at[h, i], dst_ref=rows.at[0, h, i],
            send_sem=ds_sem.at[h, i], recv_sem=dr_sem.at[h, i],
            device_id=dest(h, i), device_id_type=MESH,
        )

    def relay(h, i):
        src = slots.at[0, 0] if (h, i) == (0, 0) else rows.at[0, h, i]
        return pltpu.make_async_remote_copy(
            src_ref=src, dst_ref=rows.at[1, h, i],
            send_sem=as_sem.at[h, i], recv_sem=ar_sem.at[h, i],
            device_id=mate, device_id_type=MESH,
        )

    for h in (1, 0):
        place = (iota((TOK, TOK), 0) + TOK * h).astype(F32)
        pick = jnp.where(place == slot_row, 1.0, 0.0).astype(BF)
        slots[h, :, :CAP, :] = dot(pick, tok[...], 1, 0).astype(BF).reshape(8, CAP, D)
        slots[h, :, CAP:, :] = dot(pick, og[...], 1, 0).astype(BF).reshape(8, CAP, D)
        for i in range(8):
            if (h, i) != (0, 0):
                dispatch(h, i).start()
    relay(0, 0).start()
    rows[0, 0, 0] = slots[0, 0]
    for load in loads[2:]:
        load.wait()

    def rows_of(who, h, q):
        return pl.ds(who * 512 + (h * 2 + q) * LANES, LANES)

    def forward(who, h, q):
        here = rows_of(who, h, q)

        def body(n, acc):
            cols = pl.ds(pl.multiple_of(n * 512, 512), 512)
            feat = rows[who, h, 4 * q : 4 * q + 4, :CAP, :].reshape(LANES, D)
            scaled = rows[who, h, 4 * q : 4 * q + 4, CAP:, :].reshape(LANES, D)
            pre = dot(feat, upw[:, cols], 1, 0)
            hgrad = dot(scaled, dnw[cols, :], 1, 1)
            cdf = 0.5 * (1.0 + lax.erf(pre * SQRT_HALF))
            hid = (pre * cdf).astype(BF)
            slope = cdf + pre * jnp.exp(-0.5 * pre * pre) * INV_ROOT_TAU
            hidden[here, cols] = hid
            pregrad[here, cols] = (hgrad * slope).astype(BF)
            return acc + jnp.sum(hid.astype(F32) * hgrad, axis=1, keepdims=True)

        total = lax.fori_loop(0, 2, body, jnp.zeros((LANES, 1), F32))
        eye = iota((CAP, LANES), 0) == iota((CAP, LANES), 1)
        out = gp if who else gown
        for i in range(4):
            part = total[i * CAP : (i + 1) * CAP, :]
            row = jnp.sum(jnp.where(eye, part, 0.0), axis=0, keepdims=True)
            out[h, 4 * q + i] = jnp.broadcast_to(row, (8, LANES))

    def share_fg(h, q):
        return pltpu.make_async_remote_copy(
            src_ref=fgp.at[h, 4 * q : 4 * q + 4], dst_ref=fgr.at[h, 4 * q : 4 * q + 4],
            send_sem=fs_sem.at[h, q], recv_sem=fr_sem.at[h, q],
            device_id=mate, device_id_type=MESH,
        )

    def share_gate(h, q):
        return pltpu.make_async_remote_copy(
            src_ref=gp.at[h, 4 * q : 4 * q + 4], dst_ref=gr.at[h, 4 * q : 4 * q + 4],
            send_sem=hs_sem.at[h, q], recv_sem=hr_sem.at[h, q],
            device_id=mate, device_id_type=MESH,
        )

    def give_back(h, i):
        return pltpu.make_async_remote_copy(
            src_ref=fgs.at[h, i], dst_ref=back.at[h, i],
            send_sem=bs_sem.at[h, i], recv_sem=br_sem.at[h, i],
            device_id=source(h, i), device_id_type=MESH,
        )

    def give_gate(h, i):
        return pltpu.make_async_remote_copy(
            src_ref=ggs.at[h, i], dst_ref=ggback.at[h, i],
            send_sem=gs_sem.at[h, i], recv_sem=gr_sem.at[h, i],
            device_id=source(h, i), device_id_type=MESH,
        )

    def feature_part(who, h, q, emit):
        here = rows_of(who, h, q)

        @pl.loop(0, D // 512)
        def _(n):
            cols = pl.ds(pl.multiple_of(n * 512, 512), 512)
            emit(cols, dot(pregrad[here, :], upw[cols, :], 1, 1).reshape(4, CAP, 512))

    def mate_part(h, q):
        def emit(cols, v):
            fgp[h, 4 * q : 4 * q + 4, :, cols] = v.astype(BF)

        feature_part(1, h, q, emit)
        share_fg(h, q).start()
        share_gate(h, q).start()

    def finish(h, q):
        some = slice(4 * q, 4 * q + 4)
        share_fg(h, q).wait_recv()
        share_gate(h, q).wait_recv()

        def emit(cols, v):
            fgs[h, some, :, cols] = (v + fgr[h, some, :, cols].astype(F32)).astype(BF)

        feature_part(0, h, q, emit)
        ggs[h, some] = gown[h, some] + gr[h, some]
        for i in range(4 * q, 4 * q + 4):
            if (h, i) == (0, 0):
                back[0, 0] = fgs[0, 0]
                ggback[0, 0] = ggs[0, 0]
            else:
                give_back(h, i).start()
                give_gate(h, i).start()

    last = None
    for h, q in ((0, 0), (0, 1), (1, 0), (1, 1)):
        for i in range(4 * q, 4 * q + 4):
            if (h, i) != (0, 0):
                dispatch(h, i).wait_recv()
                relay(h, i).start()
        forward(0, h, q)
        for i in range(4 * q, 4 * q + 4):
            relay(h, i).wait_recv()
        forward(1, h, q)
        mate_part(h, q)
        if last is not None:
            finish(*last)
        last = (h, q)

    def up_pair(first, second, m, emit):
        @pl.loop(0, 4)
        def _(t):
            c, n = t // 2, t % 2
            chunk = first + c * (second - first)
            cols = pl.ds(pl.multiple_of(n * 512, 512), 512)
            feats = pl.ds(pl.multiple_of(chunk * 256 + m * LANES, LANES), LANES)
            lhs = rows[:, :, :, :CAP, feats].reshape(1024, LANES)
            emit(c, n, dot(lhs, pregrad[:, cols], 0, 0))

    def down_block(half, k, emit):
        @pl.loop(0, D // 512)
        def _(n):
            cols = pl.ds(pl.multiple_of(n * 512, 512), 512)
            feats = pl.ds(pl.multiple_of(half * 512 + k * LANES, LANES), LANES)
            rhs = rows[:, :, :, CAP:, cols].reshape(1024, 512)
            emit(cols, dot(hidden[:, feats], rhs, 0, 0))

    def ysend(t, k):
        src, dst = ((su_out, su_in), (sd_out, sd_in))[t]
        return pltpu.make_async_remote_copy(
            src_ref=src.at[k], dst_ref=dst.at[k],
            send_sem=ys_sem.at[t, k], recv_sem=yr_sem.at[t, k],
            device_id=twin, device_id_type=MESH,
        )

    def order(m, s):
        return 2 * m + (s + m) % 2

    @pl.loop(0, 2)
    def _(m):
        def emit(c, n, v):
            cols = pl.ds(pl.multiple_of((1 - n) * 512, 512), 512)
            su_out[2 * m, c, :, cols] = v[:64].astype(BF)
            su_out[2 * m + 1, c, :, cols] = v[64:].astype(BF)

        up_pair(yf, yd, m, emit)
        for s in range(2):
            ysend(0, order(m, s)).start()

    @pl.loop(0, 2)
    def _(m):
        for s in range(2):
            k = order(m, s)

            def emit(cols, v):
                sd_out[k, :, cols] = v.astype(BF)

            down_block(1, k, emit)
            ysend(1, k).start()

    finish(*last)

    zrefs = ((zu, zlu, zru), (zd, zld, zrd))

    def zright(t, k):
        src, dst, _ = zrefs[t]
        return pltpu.make_async_remote_copy(
            src_ref=src.at[k], dst_ref=dst.at[k],
            send_sem=zs_sem.at[t, k], recv_sem=zl_sem.at[t, k],
            device_id=right, device_id_type=MESH,
        )

    def zleft(t, k):
        src, _, dst = zrefs[t]
        return pltpu.make_async_remote_copy(
            src_ref=src.at[k], dst_ref=dst.at[k],
            send_sem=zs_sem.at[t, k], recv_sem=zr_sem.at[t, k],
            device_id=left, device_id_type=MESH,
        )

    def line(t, k, total, final):
        out, from_left, from_right = zrefs[t]

        @pl.when(zl == k)
        def _():
            final[...] = total[...]

        @pl.when((zl < k) & (zl == 0))
        def _():
            out[k] = total[...].astype(BF)

        @pl.when((zl < k) & (zl > 0))
        def _():
            zright(t, k).wait_recv()
            out[k] = (total[...] + from_left[k].astype(F32)).astype(BF)

        @pl.when(zl < k)
        def _():
            zright(t, k).start()

        @pl.when((zl > k) & (zl == NZ - 1))
        def _():
            out[k] = total[...].astype(BF)

        @pl.when((zl > k) & (zl < NZ - 1))
        def _():
            zleft(t, k).wait_recv()
            out[k] = (total[...] + from_right[k].astype(F32)).astype(BF)

        @pl.when(zl > k)
        def _():
            zleft(t, k).start()

    @pl.loop(0, 2)
    def _(m):
        def emit_pu(c, n, v):
            cols = pl.ds(pl.multiple_of(n * 512, 512), 512)
            pu[0, c, :, cols] = v[:64]
            pu[1, c, :, cols] = v[64:]

        up_pair(y, yr, m, emit_pu)
        for s in range(2):
            k = order(m, s)
            ysend(0, k).wait_recv()
            su[...] = pu[(s + m) % 2] + su_in[k].astype(F32)
            line(0, k, su, fu)

    def down_line(m):
        for s in range(2):
            k = 2 * m + (s + m) % 2

            def emit_sd(cols, v):
                sd[:, cols] = v

            down_block(0, k, emit_sd)
            ysend(1, k).wait_recv()
            sd[...] = sd[...] + sd_in[k].astype(F32)
            line(1, k, sd, fd)

    def settle(t, final):
        _, from_left, from_right = zrefs[t]

        @pl.when(zl > 0)
        def _():
            zright(t, zl).wait_recv()
            final[...] = final[...] + from_left[zl].astype(F32)

        @pl.when(zl < NZ - 1)
        def _():
            zleft(t, zl).wait_recv()
            final[...] = final[...] + from_right[zl].astype(F32)

    down_line(0)
    settle(0, fu)
    swap = pltpu.make_async_remote_copy(
        src_ref=fu.at[1], dst_ref=xu,
        send_sem=xs_sem.at[0], recv_sem=xr_sem.at[0],
        device_id=mate, device_id_type=MESH,
    )
    swap.start()
    down_line(1)

    for h, i in pairs:
        give_back(h, i).wait_recv()
        give_gate(h, i).wait_recv()
    spread = jnp.where(iota((TOK, 512), 1).astype(F32) == slot_col, 1.0, 0.0).astype(BF)

    @pl.loop(0, D // 512)
    def _(n):
        cols = pl.ds(pl.multiple_of(n * 512, 512), 512)
        tg_ref[:, cols] = dot(spread, back[:, :, :, cols].reshape(512, 512), 1, 0).astype(BF)

    lane = iota((TOK, LANES), 1).astype(F32)
    gate_sum = jnp.zeros((TOK, LANES), F32)
    for h in range(2):
        for i in range(8):
            base = float(h * 256 + i * CAP)
            hit = (lane < float(CAP)) & (lane + base == slot_col)
            gate_sum += jnp.where(hit, ggback[h, i, 0:1, :], 0.0)
    gate_total = jnp.sum(gate_sum, axis=1, keepdims=True) / gate_col
    eye = iota((TOK, TOK), 0) == iota((TOK, TOK), 1)
    gg_ref[...] = jnp.sum(jnp.where(eye, gate_total, 0.0), axis=0, keepdims=True).astype(BF)

    scale = 1.0 / (NY * NZ)

    def ff_chunk(c):
        return pl.ds(pl.multiple_of(c * 512, 512), 512)

    swap.wait_recv()
    ug_ref[:, ff_chunk(y)] = fu[0, :, 0:512] * scale
    ug_ref[:, ff_chunk(yf)] = fu[0, :, 512:1024] * scale
    ug_ref[:, ff_chunk(yr)] = xu[:, 0:512] * scale
    ug_ref[:, ff_chunk(yd)] = xu[:, 512:1024] * scale
    settle(1, fd)
    dg_ref[...] = fd[...] * scale

    swap.wait_send()
    relay(0, 0).wait_send()
    for h, i in pairs:
        dispatch(h, i).wait_send()
        relay(h, i).wait_send()
        give_back(h, i).wait_send()
        give_gate(h, i).wait_send()
    for h in range(2):
        for q in range(2):
            share_fg(h, q).wait_send()
            share_gate(h, q).wait_send()

    @pl.loop(0, 4)
    def _(k):
        ysend(0, k).wait_send()
        ysend(1, k).wait_send()

        @pl.when(zl != k)
        def _():
            zright(0, k).wait_send()
            zright(1, k).wait_send()


def per_device(tokens, out_grad, gate_prob, expert_id, up_weight, down_weight):
    any_spec = pl.BlockSpec(memory_space=pl.ANY)
    vmem = pl.BlockSpec(memory_space=pltpu.VMEM)
    up_blocks = pltpu.VMEM((4, 2, 64, 1024), BF)
    down_blocks = pltpu.VMEM((4, 128, D), BF)
    grads = pltpu.VMEM((2, 8, CAP, D), BF)
    gates = pltpu.VMEM((2, 8, 8, LANES), F32)
    dma = pltpu.SemaphoreType.DMA
    tg, gg, ug, dg = pl.pallas_call(
        kernel,
        out_shape=(
            jax.ShapeDtypeStruct((TOK, D), BF),
            jax.ShapeDtypeStruct((1, TOK), BF),
            jax.ShapeDtypeStruct((64, FF), F32),
            jax.ShapeDtypeStruct((128, D), F32),
        ),
        in_specs=[any_spec, any_spec, vmem, vmem, any_spec, any_spec],
        out_specs=(vmem, vmem, vmem, vmem),
        scratch_shapes=[
            pltpu.VMEM((TOK, D), BF),
            pltpu.VMEM((TOK, D), BF),
            pltpu.VMEM((D, 1024), BF),
            pltpu.VMEM((1024, D), BF),
            pltpu.VMEM((2, 8, 2 * CAP, D), BF),
            pltpu.VMEM((2, 2, 8, 2 * CAP, D), BF),
            pltpu.VMEM((1024, 1024), BF),
            pltpu.VMEM((1024, 1024), BF),
            grads, grads, grads, grads,
            gates, gates, gates, gates, gates,
            up_blocks, down_blocks, up_blocks, down_blocks, up_blocks, down_blocks,
            up_blocks, down_blocks, up_blocks, down_blocks,
            pltpu.VMEM((2, 64, 1024), F32),
            pltpu.VMEM((128, D), F32),
            pltpu.VMEM((64, 1024), F32),
            pltpu.VMEM((2, 2, 64, 1024), F32),
            pltpu.VMEM((2, 64, 1024), F32),
            pltpu.VMEM((128, D), F32),
            dma((6,)),
            dma((2, 8)), dma((2, 8)), dma((2, 8)), dma((2, 8)),
            dma((2, 2)), dma((2, 2)), dma((2, 2)), dma((2, 2)),
            dma((2, 8)), dma((2, 8)), dma((2, 8)), dma((2, 8)),
            dma((2, 4)), dma((2, 4)), dma((2, 4)), dma((2, 4)), dma((2, 4)), dma((1,)), dma((1,)),
        ],
        compiler_params=pltpu.CompilerParams(
            collective_id=0, has_side_effects=True, vmem_limit_bytes=60 * 1024 * 1024
        ),
    )(
        tokens,
        out_grad,
        gate_prob.reshape(1, TOK),
        expert_id.reshape(1, TOK),
        up_weight[0],
        down_weight[0],
    )
    return tg, gg.reshape(TOK), ug[None], dg[None]


def solution(mesh):
    return jax.shard_map(
        per_device,
        mesh=mesh,
        in_specs=(
            P(("dp", "expert"), None),
            P(("dp", "expert"), None),
            P(("dp", "expert")),
            P(("dp", "expert")),
            P("expert", None, None),
            P("expert", None, None),
        ),
        out_specs=(
            P(("dp", "expert"), None),
            P(("dp", "expert")),
            P("expert", "dp", None),
            P("expert", "dp", None),
        ),
        check_vma=False,
    )
```

time: 173 us -> 143 us (0.83)
  Pallas kernels: 164 us -> 134 us
    pallas_call x1, Pallas kernels: 164 us -> 134 us  [per_device(): pl.pallas_call(kernel, out_shape=(jax.ShapeDtypeStruct((TOK, D), BF), jax...]
where the time goes in v2:
time: 143 us; the launch traced here: 142 us
  Pallas kernels  134 us (94%)
  local copies, waits for them, and re-layouts  6.84 us (5%)
    pallas_call x1, Pallas kernels, per_device(): pl.pallas_call(kernel, out_shape=(jax.ShapeDtypeStruct((TOK, D), BF), jax...  134 us
    unnamed x3, local copies, waits for them, and re-layouts  5.62 us

profile of v2, /device:TPU:64, one launch (start us, length us, event | category | flops | bytes accessed | tf_op | source)
XLA Modules:
  0.0 142.2 jit_solution(13492907438674754710)
XLA Ops:
  0.6 1.2 reshape.17.gate_ref
  1.9 133.5 %shard_map.93 = (bf16[256,1024]{1,0:T(8,128)(2,1)}, bf16[1,256]{1,0:T(2,128)(2,1)}, f32[64,2048]{1,0:T(8,128)}, f32[128,1024]{1,0:T(8,128)}) custom-call(bf16[256,1024]{1,0:T(8,128)(2,1)} %tok_hbm.1, bf16[256,1024]{1,0:T(8,128)(2,1)} %og_hbm.1, bf16[1,256]{1,0:T(2,128)(2,1)} %reshape.17.gate_ref, s32[1,256]{1,0:T(1,128)} %bitcast.9, ...), custom_call_target="tpu_custom_call" | custom-call | tf_op jit(solution)/shard_map/pallas_call | solution.py:480
  135.4 1.2 reduce
  136.6 1.9 %copy.13 = bf16[256,1024]{1,0:T(8,128)(2,1)} copy(bf16[256,1024]{1,0:T(8,128)(2,1)} %get-tuple-element.16) | data formatting | bytes 1048576
  138.4 1.9 %copy.14 = f32[1,64,2048]{2,1,0:T(8,128)} copy(f32[1,64,2048]{2,1,0:T(8,128)} %bitcast.8) | data formatting | bytes 1048576
  140.3 1.9 %copy.15 = f32[1,128,1024]{2,1,0:T(8,128)} copy(f32[1,128,1024]{2,1,0:T(8,128)} %bitcast.7) | data formatting | bytes 1048576

commit v3 on v2

--- a/solution.py
+++ b/solution.py
@@ -38,7 +38,7 @@
     tg_ref, gg_ref, ug_ref, dg_ref,
     tok, og, upw, dnw, slots, rows, hidden, pregrad, fgp, fgr, fgs, back,
     gown, gp, gr, ggs, ggback,
-    su_out, sd_out, su_in, sd_in, zu, zd, zlu, zld, zru, zrd, fu, fd, xu, pu, su, sd,
+    su_out, sd_out, su_in, sd_in, zu, zd, zlu, zld, zru, zrd, fu, fd, xu, pu, pd,
     in_sem, ds_sem, dr_sem, as_sem, ar_sem, fs_sem, fr_sem, hs_sem, hr_sem,
     bs_sem, br_sem, gs_sem, gr_sem, ys_sem, yr_sem, zs_sem, zl_sem, zr_sem, xs_sem, xr_sem,
 ):
@@ -129,15 +129,15 @@
 
     def dispatch(h, i):
         return pltpu.make_async_remote_copy(
-            src_ref=slots.at[h, i], dst_ref=rows.at[0, h, i],
+            src_ref=slots.at[h, i], dst_ref=rows.at[h, i // 4, 0, i % 4],
             send_sem=ds_sem.at[h, i], recv_sem=dr_sem.at[h, i],
             device_id=dest(h, i), device_id_type=MESH,
         )
 
     def relay(h, i):
-        src = slots.at[0, 0] if (h, i) == (0, 0) else rows.at[0, h, i]
-        return pltpu.make_async_remote_copy(
-            src_ref=src, dst_ref=rows.at[1, h, i],
+        src = slots.at[0, 0] if (h, i) == (0, 0) else rows.at[h, i // 4, 0, i % 4]
+        return pltpu.make_async_remote_copy(
+            src_ref=src, dst_ref=rows.at[h, i // 4, 1, i % 4],
             send_sem=as_sem.at[h, i], recv_sem=ar_sem.at[h, i],
             device_id=mate, device_id_type=MESH,
         )
@@ -151,20 +151,20 @@
             if (h, i) != (0, 0):
                 dispatch(h, i).start()
     relay(0, 0).start()
-    rows[0, 0, 0] = slots[0, 0]
+    rows[0, 0, 0, 0] = slots[0, 0]
     for load in loads[2:]:
         load.wait()
 
     def rows_of(who, h, q):
-        return pl.ds(who * 512 + (h * 2 + q) * LANES, LANES)
-
-    def forward(who, h, q):
-        here = rows_of(who, h, q)
+        return pl.ds((h * 2 + q) * 256 + who * LANES, LANES)
+
+    def forward(h, q):
+        here = pl.ds((h * 2 + q) * 256, 256)
 
         def body(n, acc):
             cols = pl.ds(pl.multiple_of(n * 512, 512), 512)
-            feat = rows[who, h, 4 * q : 4 * q + 4, :CAP, :].reshape(LANES, D)
-            scaled = rows[who, h, 4 * q : 4 * q + 4, CAP:, :].reshape(LANES, D)
+            feat = rows[h, q, :, :, :CAP, :].reshape(256, D)
+            scaled = rows[h, q, :, :, CAP:, :].reshape(256, D)
             pre = dot(feat, upw[:, cols], 1, 0)
             hgrad = dot(scaled, dnw[cols, :], 1, 1)
             cdf = 0.5 * (1.0 + lax.erf(pre * SQRT_HALF))
@@ -174,13 +174,13 @@
             pregrad[here, cols] = (hgrad * slope).astype(BF)
             return acc + jnp.sum(hid.astype(F32) * hgrad, axis=1, keepdims=True)
 
-        total = lax.fori_loop(0, 2, body, jnp.zeros((LANES, 1), F32))
+        total = lax.fori_loop(0, 2, body, jnp.zeros((256, 1), F32))
         eye = iota((CAP, LANES), 0) == iota((CAP, LANES), 1)
-        out = gp if who else gown
-        for i in range(4):
-            part = total[i * CAP : (i + 1) * CAP, :]
-            row = jnp.sum(jnp.where(eye, part, 0.0), axis=0, keepdims=True)
-            out[h, 4 * q + i] = jnp.broadcast_to(row, (8, LANES))
+        for who, out in ((0, gown), (1, gp)):
+            for i in range(4):
+                part = total[who * LANES + i * CAP : who * LANES + (i + 1) * CAP, :]
+                row = jnp.sum(jnp.where(eye, part, 0.0), axis=0, keepdims=True)
+                out[h, 4 * q + i] = jnp.broadcast_to(row, (8, LANES))
 
     def share_fg(h, q):
         return pltpu.make_async_remote_copy(
@@ -250,32 +250,31 @@
             if (h, i) != (0, 0):
                 dispatch(h, i).wait_recv()
                 relay(h, i).start()
-        forward(0, h, q)
+        if last is not None:
+            finish(*last)
         for i in range(4 * q, 4 * q + 4):
             relay(h, i).wait_recv()
-        forward(1, h, q)
+        forward(h, q)
         mate_part(h, q)
-        if last is not None:
-            finish(*last)
         last = (h, q)
 
-    def up_pair(first, second, m, emit):
-        @pl.loop(0, 4)
-        def _(t):
-            c, n = t // 2, t % 2
+    def up_part(first, second, emit):
+        @pl.loop(0, 2)
+        def _(c):
             chunk = first + c * (second - first)
-            cols = pl.ds(pl.multiple_of(n * 512, 512), 512)
-            feats = pl.ds(pl.multiple_of(chunk * 256 + m * LANES, LANES), LANES)
-            lhs = rows[:, :, :, :CAP, feats].reshape(1024, LANES)
-            emit(c, n, dot(lhs, pregrad[:, cols], 0, 0))
-
-    def down_block(half, k, emit):
-        @pl.loop(0, D // 512)
-        def _(n):
-            cols = pl.ds(pl.multiple_of(n * 512, 512), 512)
-            feats = pl.ds(pl.multiple_of(half * 512 + k * LANES, LANES), LANES)
-            rhs = rows[:, :, :, CAP:, cols].reshape(1024, 512)
-            emit(cols, dot(hidden[:, feats], rhs, 0, 0))
+            feats = pl.ds(pl.multiple_of(chunk * 256, 256), 256)
+            lhs = rows[:, :, :, :, :CAP, feats].reshape(1024, 256).T
+            for n in range(2):
+                emit(c, n, dot(lhs, pregrad[:, n * 512 : n * 512 + 512], 1, 0))
+
+    def down_part(half, emit):
+        @pl.loop(0, 2)
+        def _(m):
+            feats = pl.ds(pl.multiple_of(half * 512 + m * 256, 256), 256)
+            lhs = hidden[:, feats].T
+            for n in range(2):
+                rhs = rows[:, :, :, :, CAP:, n * 512 : n * 512 + 512].reshape(1024, 512)
+                emit(m, n, dot(lhs, rhs, 1, 0))
 
     def ysend(t, k):
         src, dst = ((su_out, su_in), (sd_out, sd_in))[t]
@@ -285,32 +284,27 @@
             device_id=twin, device_id_type=MESH,
         )
 
-    def order(m, s):
-        return 2 * m + (s + m) % 2
-
-    @pl.loop(0, 2)
-    def _(m):
-        def emit(c, n, v):
-            cols = pl.ds(pl.multiple_of((1 - n) * 512, 512), 512)
-            su_out[2 * m, c, :, cols] = v[:64].astype(BF)
-            su_out[2 * m + 1, c, :, cols] = v[64:].astype(BF)
-
-        up_pair(yf, yd, m, emit)
+    low = 1 - zl // 2
+
+    def block(n):
+        k = n // 2 + (n % 2) * (3 - 2 * (n // 2))
+        return k + low * (3 - 2 * k)
+
+    def emit_up_out(c, n, v):
+        for k in range(4):
+            su_out[k, c, :, (1 - n) * 512 : (2 - n) * 512] = v[64 * k : 64 * k + 64].astype(BF)
+
+    def emit_up_own(c, n, v):
+        for k in range(4):
+            pu[k, c, :, n * 512 : n * 512 + 512] = v[64 * k : 64 * k + 64]
+
+    def emit_down_out(m, n, v):
         for s in range(2):
-            ysend(0, order(m, s)).start()
-
-    @pl.loop(0, 2)
-    def _(m):
+            sd_out[2 * m + s, :, n * 512 : n * 512 + 512] = v[128 * s : 128 * s + 128].astype(BF)
+
+    def emit_down_own(m, n, v):
         for s in range(2):
-            k = order(m, s)
-
-            def emit(cols, v):
-                sd_out[k, :, cols] = v.astype(BF)
-
-            down_block(1, k, emit)
-            ysend(1, k).start()
-
-    finish(*last)
+            pd[2 * m + s, :, n * 512 : n * 512 + 512] = v[128 * s : 128 * s + 128]
 
     zrefs = ((zu, zlu, zru), (zd, zld, zrd))
 
@@ -363,31 +357,38 @@
         def _():
             zleft(t, k).start()
 
-    @pl.loop(0, 2)
-    def _(m):
-        def emit_pu(c, n, v):
-            cols = pl.ds(pl.multiple_of(n * 512, 512), 512)
-            pu[0, c, :, cols] = v[:64]
-            pu[1, c, :, cols] = v[64:]
-
-        up_pair(y, yr, m, emit_pu)
-        for s in range(2):
-            k = order(m, s)
-            ysend(0, k).wait_recv()
-            su[...] = pu[(s + m) % 2] + su_in[k].astype(F32)
-            line(0, k, su, fu)
-
-    def down_line(m):
-        for s in range(2):
-            k = 2 * m + (s + m) % 2
-
-            def emit_sd(cols, v):
-                sd[:, cols] = v
-
-            down_block(0, k, emit_sd)
-            ysend(1, k).wait_recv()
-            sd[...] = sd[...] + sd_in[k].astype(F32)
-            line(1, k, sd, fd)
+    def step(t, n):
+        k = block(n)
+        own, came = ((pu, su_in), (pd, sd_in))[t]
+        ysend(t, k).wait_recv()
+        own[k] = own[k] + came[k].astype(F32)
+        line(t, k, own.at[k], (fu, fd)[t])
+
+    edge = (zl == 0) | (zl == NZ - 1)
+
+    up_part(yf, yd, emit_up_out)
+    for n in range(4):
+        ysend(0, block(n)).start()
+    up_part(y, yr, emit_up_own)
+
+    @pl.when(edge)
+    def _():
+        step(0, 0)
+
+    finish(*last)
+    down_part(1, emit_down_out)
+    for n in range(4):
+        ysend(1, block(n)).start()
+
+    @pl.when(jnp.logical_not(edge))
+    def _():
+        step(0, 0)
+
+    down_part(0, emit_down_own)
+
+    @pl.loop(1, 4)
+    def _(n):
+        step(0, n)
 
     def settle(t, final):
         _, from_left, from_right = zrefs[t]
@@ -402,7 +403,8 @@
             zleft(t, zl).wait_recv()
             final[...] = final[...] + from_right[zl].astype(F32)
 
-    down_line(0)
+    for n in range(2):
+        step(1, n)
     settle(0, fu)
     swap = pltpu.make_async_remote_copy(
         src_ref=fu.at[1], dst_ref=xu,
@@ -410,7 +412,8 @@
         device_id=mate, device_id_type=MESH,
     )
     swap.start()
-    down_line(1)
+    for n in range(2, 4):
+        step(1, n)
 
     for h, i in pairs:
         give_back(h, i).wait_recv()
@@ -467,6 +470,20 @@
         def _():
             zright(0, k).wait_send()
             zright(1, k).wait_send()
+
+
+def tail(tg_in, gg_in, ug_in, dg_in, tg_out, gg_out, ug_out, dg_out, tg, ug, dg, sem_in, sem_out):
+    moves = ((tg_in, tg, tg_out), (ug_in, ug, ug_out), (dg_in, dg, dg_out))
+    ins = [pltpu.make_async_copy(a, b, sem_in.at[n]) for n, (a, b, _) in enumerate(moves)]
+    outs = [pltpu.make_async_copy(b, c, sem_out.at[n]) for n, (_, b, c) in enumerate(moves)]
+    for copy in ins:
+        copy.start()
+    gg_out[...] = gg_in[...]
+    for arrive, leave in zip(ins, outs):
+        arrive.wait()
+        leave.start()
+    for leave in outs:
+        leave.wait()
 
 
 def per_device(tokens, out_grad, gate_prob, expert_id, up_weight, down_weight):
@@ -493,7 +510,7 @@
             pltpu.VMEM((D, 1024), BF),
             pltpu.VMEM((1024, D), BF),
             pltpu.VMEM((2, 8, 2 * CAP, D), BF),
-            pltpu.VMEM((2, 2, 8, 2 * CAP, D), BF),
+            pltpu.VMEM((2, 2, 2, 4, 2 * CAP, D), BF),
             pltpu.VMEM((1024, 1024), BF),
             pltpu.VMEM((1024, 1024), BF),
             grads, grads, grads, grads,
@@ -503,9 +520,8 @@
             pltpu.VMEM((2, 64, 1024), F32),
             pltpu.VMEM((128, D), F32),
             pltpu.VMEM((64, 1024), F32),
-            pltpu.VMEM((2, 2, 64, 1024), F32),
-            pltpu.VMEM((2, 64, 1024), F32),
-            pltpu.VMEM((128, D), F32),
+            pltpu.VMEM((4, 2, 64, 1024), F32),
+            pltpu.VMEM((4, 128, D), F32),
             dma((6,)),
             dma((2, 8)), dma((2, 8)), dma((2, 8)), dma((2, 8)),
             dma((2, 2)), dma((2, 2)), dma((2, 2)), dma((2, 2)),
@@ -523,6 +539,24 @@
         up_weight[0],
         down_weight[0],
     )
+    tg, gg, ug, dg = pl.pallas_call(
+        tail,
+        out_shape=(
+            jax.ShapeDtypeStruct((TOK, D), BF),
+            jax.ShapeDtypeStruct((1, TOK), BF),
+            jax.ShapeDtypeStruct((64, FF), F32),
+            jax.ShapeDtypeStruct((128, D), F32),
+        ),
+        in_specs=[any_spec, vmem, any_spec, any_spec],
+        out_specs=(any_spec, vmem, any_spec, any_spec),
+        scratch_shapes=[
+            pltpu.VMEM((TOK, D), BF),
+            pltpu.VMEM((64, FF), F32),
+            pltpu.VMEM((128, D), F32),
+            dma((3,)),
+            dma((3,)),
+        ],
+    )(tg, gg, ug, dg)
     return tg, gg.reshape(TOK), ug[None], dg[None]
 
 

time: 143 us -> 129 us (0.902)
  Pallas kernels: 134 us -> 124 us
  local copies, waits for them, and re-layouts: 6.84 us -> 1.22 us
    pallas_call x1, Pallas kernels: 134 us -> 121 us  [per_device(): pl.pallas_call(kernel, out_shape=(jax.ShapeDtypeStruct((TOK, D), BF), jax...]
    unnamed x3 -> x0, local copies, waits for them, and re-layouts: 5.62 us -> none
    pallas_call x0 -> x1, Pallas kernels: none -> 3.47 us  [per_device(): pl.pallas_call(tail, out_shape=(jax.ShapeDtypeStruct((TOK, D), BF), jax.S...]
where the time goes in v3:
time: 129 us; the launch traced here: 127 us
  Pallas kernels  124 us (96%)
    pallas_call x1, Pallas kernels, per_device(): pl.pallas_call(kernel, out_shape=(jax.ShapeDtypeStruct((TOK, D), BF), jax...  121 us
    pallas_call x1, Pallas kernels, per_device(): pl.pallas_call(tail, out_shape=(jax.ShapeDtypeStruct((TOK, D), BF), jax.S...  3.47 us

profile of v3, /device:TPU:64, one launch (start us, length us, event | category | flops | bytes accessed | tf_op | source)
XLA Modules:
  0.0 127.2 jit_solution(94582380045843420)
XLA Ops:
  0.6 1.2 reshape.17.gate_ref
  1.9 120.7 %shard_map.93 = (bf16[256,1024]{1,0:T(8,128)(2,1)}, bf16[1,256]{1,0:T(2,128)(2,1)}, f32[64,2048]{1,0:T(8,128)}, f32[128,1024]{1,0:T(8,128)}) custom-call(bf16[256,1024]{1,0:T(8,128)(2,1)} %tok_hbm.1, bf16[256,1024]{1,0:T(8,128)(2,1)} %og_hbm.1, bf16[1,256]{1,0:T(2,128)(2,1)} %reshape.17.gate_ref, s32[1,256]{1,0:T(1,128)} %bitcast.7, ...), custom_call_target="tpu_custom_call" | custom-call | tf_op jit(solution)/shard_map/pallas_call | solution.py:497
  122.5 3.5 %shard_map.94 = (bf16[256,1024]{1,0:T(8,128)(2,1)}, bf16[1,256]{1,0:T(2,128)(2,1)}, f32[64,2048]{1,0:T(8,128)}, f32[128,1024]{1,0:T(8,128)}) custom-call(bf16[256,1024]{1,0:T(8,128)(2,1)} %get-tuple-element.12.tg_in, bf16[1,256]{1,0:T(2,128)(2,1)} %get-tuple-element.13.gg_in, f32[64,2048]{1,0:T(8,128)} %get-tuple-element.14.ug_in, ...), custom_call_target="tpu_custom_call" | custom-call | tf_op jit(solution)/shard_map/pallas_call | solution.py:542
  126.0 1.2 reduce

commit v4 on v3

--- a/solution.py
+++ b/solution.py
@@ -17,6 +17,7 @@
 NY = 4
 NZ = 4
 LANES = 128
+AWAY = (0, 1, 2, 3, 6, 7, 4, 5)
 
 
 def dot(a, b, ca, cb):
@@ -60,10 +61,10 @@
         return ((1 - zh) if h else zh) * 8 + other
 
     def dest(h, i):
-        return (group_dp(h), group_ex(h, (j + i) % 8))
+        return (group_dp(h), group_ex(h, (j + AWAY[i]) % 8))
 
     def source(h, i):
-        return (group_dp(h), group_ex(h, (j + 8 - i) % 8))
+        return (group_dp(h), group_ex(h, (j + 8 - AWAY[i]) % 8))
 
     mate = (yr * NZ + zl, ex)
     twin = (yf * NZ + zl, ex)
@@ -113,6 +114,7 @@
         half = jnp.where(ident >= 8.0, 1.0, 0.0)
         rank = ident - 8.0 * half - j.astype(F32)
         rank = jnp.where(rank < 0.0, rank + 8.0, rank)
+        rank = rank + jnp.where(rank >= 6.0, -2.0, jnp.where(rank >= 4.0, 2.0, 0.0))
         cross = jnp.abs(half - mine)
         return cross * 256.0 + rank * 32.0 + place
 
@@ -129,15 +131,15 @@
 
     def dispatch(h, i):
         return pltpu.make_async_remote_copy(
-            src_ref=slots.at[h, i], dst_ref=rows.at[h, i // 4, 0, i % 4],
+            src_ref=slots.at[h, i], dst_ref=rows.at[h, i // 2, 0, i % 2],
             send_sem=ds_sem.at[h, i], recv_sem=dr_sem.at[h, i],
             device_id=dest(h, i), device_id_type=MESH,
         )
 
     def relay(h, i):
-        src = slots.at[0, 0] if (h, i) == (0, 0) else rows.at[h, i // 4, 0, i % 4]
-        return pltpu.make_async_remote_copy(
-            src_ref=src, dst_ref=rows.at[h, i // 4, 1, i % 4],
+        src = slots.at[0, 0] if (h, i) == (0, 0) else rows.at[h, i // 2, 0, i % 2]
+        return pltpu.make_async_remote_copy(
+            src_ref=src, dst_ref=rows.at[h, i // 2, 1, i % 2],
             send_sem=as_sem.at[h, i], recv_sem=ar_sem.at[h, i],
             device_id=mate, device_id_type=MESH,
         )
@@ -155,16 +157,15 @@
     for load in loads[2:]:
         load.wait()
 
-    def rows_of(who, h, q):
-        return pl.ds((h * 2 + q) * 256 + who * LANES, LANES)
-
-    def forward(h, q):
-        here = pl.ds((h * 2 + q) * 256, 256)
-
-        def body(n, acc):
-            cols = pl.ds(pl.multiple_of(n * 512, 512), 512)
-            feat = rows[h, q, :, :, :CAP, :].reshape(256, D)
-            scaled = rows[h, q, :, :, CAP:, :].reshape(256, D)
+    def forward(h, first, count):
+        size = count * 2 * CAP
+        here = pl.ds((h * 8 + first) * 2 * CAP, size)
+        some = slice(first // 2, (first + count) // 2)
+        total = jnp.zeros((size, 1), F32)
+        for n in range(2):
+            cols = slice(n * 512, n * 512 + 512)
+            feat = rows[h, some, :, :, :CAP, :].reshape(size, D)
+            scaled = rows[h, some, :, :, CAP:, :].reshape(size, D)
             pre = dot(feat, upw[:, cols], 1, 0)
             hgrad = dot(scaled, dnw[cols, :], 1, 1)
             cdf = 0.5 * (1.0 + lax.erf(pre * SQRT_HALF))
@@ -172,15 +173,15 @@
             slope = cdf + pre * jnp.exp(-0.5 * pre * pre) * INV_ROOT_TAU
             hidden[here, cols] = hid
             pregrad[here, cols] = (hgrad * slope).astype(BF)
-            return acc + jnp.sum(hid.astype(F32) * hgrad, axis=1, keepdims=True)
-
-        total = lax.fori_loop(0, 2, body, jnp.zeros((256, 1), F32))
+            total += jnp.sum(hid.astype(F32) * hgrad, axis=1, keepdims=True)
         eye = iota((CAP, LANES), 0) == iota((CAP, LANES), 1)
-        for who, out in ((0, gown), (1, gp)):
-            for i in range(4):
-                part = total[who * LANES + i * CAP : who * LANES + (i + 1) * CAP, :]
-                row = jnp.sum(jnp.where(eye, part, 0.0), axis=0, keepdims=True)
-                out[h, 4 * q + i] = jnp.broadcast_to(row, (8, LANES))
+        for pair in range(count // 2):
+            for who, out in ((0, gown), (1, gp)):
+                for i in range(2):
+                    start = (pair * 4 + who * 2 + i) * CAP
+                    part = total[start : start + CAP, :]
+                    row = jnp.sum(jnp.where(eye, part, 0.0), axis=0, keepdims=True)
+                    out[h, first + 2 * pair + i] = jnp.broadcast_to(row, (8, LANES))
 
     def share_fg(h, q):
         return pltpu.make_async_remote_copy(
@@ -211,12 +212,14 @@
         )
 
     def feature_part(who, h, q, emit):
-        here = rows_of(who, h, q)
-
         @pl.loop(0, D // 512)
         def _(n):
             cols = pl.ds(pl.multiple_of(n * 512, 512), 512)
-            emit(cols, dot(pregrad[here, :], upw[cols, :], 1, 1).reshape(4, CAP, 512))
+            base = (h * 8 + 4 * q) * 2 * CAP + who * 2 * CAP
+            lhs = jnp.concatenate(
+                [pregrad[pl.ds(base + p * 4 * CAP, 2 * CAP), :] for p in range(2)], axis=0
+            )
+            emit(cols, dot(lhs, upw[cols, :], 1, 1).reshape(4, CAP, 512))
 
     def mate_part(h, q):
         def emit(cols, v):
@@ -246,17 +249,26 @@
 
     last = None
     for h, q in ((0, 0), (0, 1), (1, 0), (1, 1)):
-        for i in range(4 * q, 4 * q + 4):
-            if (h, i) != (0, 0):
-                dispatch(h, i).wait_recv()
-                relay(h, i).start()
-        if last is not None:
-            finish(*last)
-        for i in range(4 * q, 4 * q + 4):
-            relay(h, i).wait_recv()
-        forward(h, q)
-        mate_part(h, q)
+        final = (h, q) == (1, 1)
+        for first, count in ((4 * q, 2), (4 * q + 2, 2)) if final else ((4 * q, 4),):
+            for i in range(first, first + count):
+                if (h, i) != (0, 0):
+                    dispatch(h, i).wait_recv()
+                    relay(h, i).start()
+            if last is not None and first == 4 * q:
+                finish(*last)
+            for i in range(first, first + count):
+                relay(h, i).wait_recv()
+            forward(h, first, count)
+        if not final:
+            mate_part(h, q)
         last = (h, q)
+
+    low = 1 - zl // 2
+
+    def block(n):
+        k = n // 2 + (n % 2) * (3 - 2 * (n // 2))
+        return k + low * (3 - 2 * k)
 
     def up_part(first, second, emit):
         @pl.loop(0, 2)
@@ -267,14 +279,20 @@
             for n in range(2):
                 emit(c, n, dot(lhs, pregrad[:, n * 512 : n * 512 + 512], 1, 0))
 
-    def down_part(half, emit):
-        @pl.loop(0, 2)
-        def _(m):
-            feats = pl.ds(pl.multiple_of(half * 512 + m * 256, 256), 256)
-            lhs = hidden[:, feats].T
-            for n in range(2):
-                rhs = rows[:, :, :, :, CAP:, n * 512 : n * 512 + 512].reshape(1024, 512)
-                emit(m, n, dot(lhs, rhs, 1, 0))
+    def down_part(half, n0, emit):
+        blocks = (block(n0), block(n0 + 1))
+        lhs = jnp.concatenate(
+            [
+                hidden[:, pl.ds(pl.multiple_of(half * 512 + k * LANES, LANES), LANES)].T
+                for k in blocks
+            ],
+            axis=0,
+        )
+        for n in range(2):
+            rhs = rows[:, :, :, :, CAP:, n * 512 : n * 512 + 512].reshape(1024, 512)
+            v = dot(lhs, rhs, 1, 0)
+            emit(blocks[0], n, v[:LANES])
+            emit(blocks[1], n, v[LANES:])
 
     def ysend(t, k):
         src, dst = ((su_out, su_in), (sd_out, sd_in))[t]
@@ -284,12 +302,6 @@
             device_id=twin, device_id_type=MESH,
         )
 
-    low = 1 - zl // 2
-
-    def block(n):
-        k = n // 2 + (n % 2) * (3 - 2 * (n // 2))
-        return k + low * (3 - 2 * k)
-
     def emit_up_out(c, n, v):
         for k in range(4):
             su_out[k, c, :, (1 - n) * 512 : (2 - n) * 512] = v[64 * k : 64 * k + 64].astype(BF)
@@ -298,13 +310,11 @@
         for k in range(4):
             pu[k, c, :, n * 512 : n * 512 + 512] = v[64 * k : 64 * k + 64]
 
-    def emit_down_out(m, n, v):
-        for s in range(2):
-            sd_out[2 * m + s, :, n * 512 : n * 512 + 512] = v[128 * s : 128 * s + 128].astype(BF)
-
-    def emit_down_own(m, n, v):
-        for s in range(2):
-            pd[2 * m + s, :, n * 512 : n * 512 + 512] = v[128 * s : 128 * s + 128]
+    def emit_down_out(k, n, v):
+        sd_out[k, :, n * 512 : n * 512 + 512] = v.astype(BF)
+
+    def emit_down_own(k, n, v):
+        pd[k, :, n * 512 : n * 512 + 512] = v
 
     zrefs = ((zu, zlu, zru), (zd, zld, zrd))
 
@@ -366,30 +376,39 @@
 
     edge = (zl == 0) | (zl == NZ - 1)
 
+    down_part(1, 0, emit_down_out)
+    for n in range(2):
+        ysend(1, block(n)).start()
+    down_part(0, 0, emit_down_own)
+    mate_part(1, 1)
+
+    @pl.when(edge)
+    def _():
+        step(1, 0)
+
     up_part(yf, yd, emit_up_out)
     for n in range(4):
         ysend(0, block(n)).start()
+    finish(*last)
     up_part(y, yr, emit_up_own)
-
-    @pl.when(edge)
-    def _():
-        step(0, 0)
-
-    finish(*last)
-    down_part(1, emit_down_out)
-    for n in range(4):
-        ysend(1, block(n)).start()
 
     @pl.when(jnp.logical_not(edge))
     def _():
-        step(0, 0)
-
-    down_part(0, emit_down_own)
+        step(1, 0)
+
+    step(1, 1)
+    step(0, 0)
+    down_part(1, 2, emit_down_out)
+    for n in range(2, 4):
+        ysend(1, block(n)).start()
+    down_part(0, 2, emit_down_own)
 
     @pl.loop(1, 4)
     def _(n):
         step(0, n)
 
+    step(1, 2)
+
     def settle(t, final):
         _, from_left, from_right = zrefs[t]
 
@@ -403,8 +422,6 @@
             zleft(t, zl).wait_recv()
             final[...] = final[...] + from_right[zl].astype(F32)
 
-    for n in range(2):
-        step(1, n)
     settle(0, fu)
     swap = pltpu.make_async_remote_copy(
         src_ref=fu.at[1], dst_ref=xu,
@@ -412,8 +429,7 @@
         device_id=mate, device_id_type=MESH,
     )
     swap.start()
-    for n in range(2, 4):
-        step(1, n)
+    step(1, 3)
 
     for h, i in pairs:
         give_back(h, i).wait_recv()
@@ -510,7 +526,7 @@
             pltpu.VMEM((D, 1024), BF),
             pltpu.VMEM((1024, D), BF),
             pltpu.VMEM((2, 8, 2 * CAP, D), BF),
-            pltpu.VMEM((2, 2, 2, 4, 2 * CAP, D), BF),
+            pltpu.VMEM((2, 4, 2, 2, 2 * CAP, D), BF),
             pltpu.VMEM((1024, 1024), BF),
             pltpu.VMEM((1024, 1024), BF),
             grads, grads, grads, grads,

time: 129 us -> 130 us (level)
  Pallas kernels: 124 us -> 126 us
    pallas_call x1, Pallas kernels: 121 us -> 122 us  [per_device(): pl.pallas_call(kernel, out_shape=(jax.ShapeDtypeStruct((TOK, D), BF), jax...]
where the time goes in v4:
time: 130 us; the launch traced here: 129 us
  Pallas kernels  126 us (97%)
    pallas_call x1, Pallas kernels, per_device(): pl.pallas_call(kernel, out_shape=(jax.ShapeDtypeStruct((TOK, D), BF), jax...  122 us
    pallas_call x1, Pallas kernels, per_device(): pl.pallas_call(tail, out_shape=(jax.ShapeDtypeStruct((TOK, D), BF), jax.S...  3.47 us

profile of v4, /device:TPU:64, one launch (start us, length us, event | category | flops | bytes accessed | tf_op | source)
XLA Modules:
  0.0 128.6 jit_solution(6286519806889204960)
XLA Ops:
  0.6 1.2 reshape.17.gate_ref
  1.9 122.1 %shard_map.93 = (bf16[256,1024]{1,0:T(8,128)(2,1)}, bf16[1,256]{1,0:T(2,128)(2,1)}, f32[64,2048]{1,0:T(8,128)}, f32[128,1024]{1,0:T(8,128)}) custom-call(bf16[256,1024]{1,0:T(8,128)(2,1)} %tok_hbm.1, bf16[256,1024]{1,0:T(8,128)(2,1)} %og_hbm.1, bf16[1,256]{1,0:T(2,128)(2,1)} %reshape.17.gate_ref, s32[1,256]{1,0:T(1,128)} %bitcast.7, ...), custom_call_target="tpu_custom_call" | custom-call | tf_op jit(solution)/shard_map/pallas_call | solution.py:513
  123.9 3.5 %shard_map.94 = (bf16[256,1024]{1,0:T(8,128)(2,1)}, bf16[1,256]{1,0:T(2,128)(2,1)}, f32[64,2048]{1,0:T(8,128)}, f32[128,1024]{1,0:T(8,128)}) custom-call(bf16[256,1024]{1,0:T(8,128)(2,1)} %get-tuple-element.12.tg_in, bf16[1,256]{1,0:T(2,128)(2,1)} %get-tuple-element.13.gg_in, f32[64,2048]{1,0:T(8,128)} %get-tuple-element.14.ug_in, ...), custom_call_target="tpu_custom_call" | custom-call | tf_op jit(solution)/shard_map/pallas_call | solution.py:558
  127.4 1.2 reduce

commit v5 on v3

--- a/solution.py
+++ b/solution.py
@@ -118,7 +118,7 @@
 
     slot_row = slot_of(ids_row, pos_row)
     slot_col = slot_of(ids_col, pos_col)
-    gate_row = gate_ref[...].astype(F32)
+    gate_row = gate_ref[...].astype(F32).reshape(1, TOK)
     gate_col = to_column(gate_row)
 
     loads[0].wait()
@@ -472,18 +472,14 @@
             zright(1, k).wait_send()
 
 
-def tail(tg_in, gg_in, ug_in, dg_in, tg_out, gg_out, ug_out, dg_out, tg, ug, dg, sem_in, sem_out):
-    moves = ((tg_in, tg, tg_out), (ug_in, ug, ug_out), (dg_in, dg, dg_out))
-    ins = [pltpu.make_async_copy(a, b, sem_in.at[n]) for n, (a, b, _) in enumerate(moves)]
-    outs = [pltpu.make_async_copy(b, c, sem_out.at[n]) for n, (_, b, c) in enumerate(moves)]
-    for copy in ins:
+def tail(tg_in, gg_in, ug_in, dg_in, tg_out, gg_out, ug_out, dg_out, sem):
+    moves = ((tg_in, tg_out), (ug_in, ug_out), (dg_in, dg_out))
+    copies = [pltpu.make_async_copy(a, b, sem.at[n]) for n, (a, b) in enumerate(moves)]
+    for copy in copies:
         copy.start()
-    gg_out[...] = gg_in[...]
-    for arrive, leave in zip(ins, outs):
-        arrive.wait()
-        leave.start()
-    for leave in outs:
-        leave.wait()
+    gg_out[...] = gg_in[...].reshape(TOK)
+    for copy in copies:
+        copy.wait()
 
 
 def per_device(tokens, out_grad, gate_prob, expert_id, up_weight, down_weight):
@@ -529,12 +525,12 @@
             dma((2, 4)), dma((2, 4)), dma((2, 4)), dma((2, 4)), dma((2, 4)), dma((1,)), dma((1,)),
         ],
         compiler_params=pltpu.CompilerParams(
-            collective_id=0, has_side_effects=True, vmem_limit_bytes=60 * 1024 * 1024
+            collective_id=0, has_side_effects=True, vmem_limit_bytes=50 * 1024 * 1024
         ),
     )(
         tokens,
         out_grad,
-        gate_prob.reshape(1, TOK),
+        gate_prob,
         expert_id.reshape(1, TOK),
         up_weight[0],
         down_weight[0],
@@ -543,21 +539,18 @@
         tail,
         out_shape=(
             jax.ShapeDtypeStruct((TOK, D), BF),
-            jax.ShapeDtypeStruct((1, TOK), BF),
+            jax.ShapeDtypeStruct((TOK,), BF),
             jax.ShapeDtypeStruct((64, FF), F32),
             jax.ShapeDtypeStruct((128, D), F32),
         ),
-        in_specs=[any_spec, vmem, any_spec, any_spec],
+        in_specs=[vmem, vmem, vmem, vmem],
         out_specs=(any_spec, vmem, any_spec, any_spec),
         scratch_shapes=[
-            pltpu.VMEM((TOK, D), BF),
-            pltpu.VMEM((64, FF), F32),
-            pltpu.VMEM((128, D), F32),
-            dma((3,)),
             dma((3,)),
         ],
+        compiler_params=pltpu.CompilerParams(vmem_limit_bytes=2 * 1024 * 1024),
     )(tg, gg, ug, dg)
-    return tg, gg.reshape(TOK), ug[None], dg[None]
+    return tg, gg, ug[None], dg[None]
 
 
 def solution(mesh):

time: 129 us -> 127 us (0.984)
  Pallas kernels: 124 us -> 121 us
  local copies, waits for them, and re-layouts: 1.22 us -> 3.41 us
    unnamed x0 -> x8, local copies, waits for them, and re-layouts: none -> 3.41 us
    pallas_call x1, Pallas kernels: 3.47 us -> 1.68 us  [per_device(): pl.pallas_call(tail, out_shape=(jax.ShapeDtypeStruct((TOK, D), BF), jax.S...]
    pallas_call x1, Pallas kernels: 121 us -> 119 us  [per_device(): pl.pallas_call(kernel, out_shape=(jax.ShapeDtypeStruct((TOK, D), BF), jax...]
where the time goes in v5:
time: 127 us; the launch traced here: 125 us
  Pallas kernels  121 us (95%)
  local copies, waits for them, and re-layouts  3.41 us (3%)
    pallas_call x1, Pallas kernels, per_device(): pl.pallas_call(kernel, out_shape=(jax.ShapeDtypeStruct((TOK, D), BF), jax...  119 us
    unnamed x8, local copies, waits for them, and re-layouts  3.41 us

profile of v5, /device:TPU:64, one launch (start us, length us, event | category | flops | bytes accessed | tf_op | source)
XLA Modules:
  0.0 124.9 jit_solution(4000428628880056938)
XLA Ops:
  0.6 0.0 copy-start
  0.6 1.0 copy-done
  1.7 0.0 copy-start.1
  1.7 1.0 copy-done.1
  2.7 0.0 copy-start.2
  2.7 0.7 copy-done.2
  3.4 0.0 copy-start.3
  3.4 0.7 copy-done.3
  4.1 119.2 %shard_map.93 = (bf16[256,1024]{1,0:T(8,128)(2,1)S(1)}, bf16[1,256]{1,0:T(2,128)(2,1)S(1)}, f32[64,2048]{1,0:T(8,128)S(1)}, f32[128,1024]{1,0:T(8,128)S(1)}) custom-call(bf16[256,1024]{1,0:T(8,128)(2,1)S(1)} %copy-done, bf16[256,1024]{1,0:T(8,128)(2,1)S(1)} %copy-done.1, bf16[256]{0:T(256)(128)(2,1)S(1)} %copy-done.3, s32[1,256]{1,0:T(1,128)S(1)} %bitcast.5, ...), custom_call_target="tpu_custom_call" | custom-call | tf_op jit(solution)/shard_map/pallas_call | solution.py:493
  123.2 1.7 %shard_map.94 = (bf16[256,1024]{1,0:T(8,128)(2,1)}, bf16[256]{0:T(256)(128)(2,1)}, f32[64,2048]{1,0:T(8,128)}, f32[128,1024]{1,0:T(8,128)}) custom-call(bf16[256,1024]{1,0:T(8,128)(2,1)S(1)} %get-tuple-element.12.tg_in, bf16[1,256]{1,0:T(2,128)(2,1)S(1)} %get-tuple-element.13.gg_in, f32[64,2048]{1,0:T(8,128)S(1)} %get-tuple-element.14.ug_in, ...), custom_call_target="tpu_custom_call" | custom-call | tf_op jit(solution)/shard_map/pallas_call | solution.py:538
Async XLA Ops:
  0.6 1.0 copy-start
  1.7 1.0 copy-start.1
  2.7 0.7 copy-start.2
  3.4 0.7 copy-start.3

commit v6 on v5

--- a/solution.py
+++ b/solution.py
@@ -34,9 +34,9 @@
 
 
 def kernel(
-    tok_hbm, og_hbm, gate_ref, id_ref, upw_hbm, dnw_hbm,
+    tok_hbm, og_hbm, gate_hbm, id_hbm, upw_hbm, dnw_hbm,
     tg_ref, gg_ref, ug_ref, dg_ref,
-    tok, og, upw, dnw, slots, rows, hidden, pregrad, fgp, fgr, fgs, back,
+    gate_ref, id_ref, tok, og, upw, dnw, slots, rows, hidden, pregrad, fgp, fgr, fgs, back,
     gown, gp, gr, ggs, ggback,
     su_out, sd_out, su_in, sd_in, zu, zd, zlu, zld, zru, zrd, fu, fd, xu, pu, pd,
     in_sem, ds_sem, dr_sem, as_sem, ar_sem, fs_sem, fr_sem, hs_sem, hr_sem,
@@ -72,6 +72,8 @@
     pairs = [(h, i) for h in (1, 0) for i in range(8) if (h, i) != (0, 0)]
 
     sources = [
+        (id_hbm, id_ref),
+        (gate_hbm, gate_ref),
         (tok_hbm, tok),
         (og_hbm, og),
         (upw_hbm.at[:, pl.ds(pl.multiple_of(y * 512, 512), 512)], upw.at[:, 0:512]),
@@ -99,6 +101,8 @@
     def _():
         pl.semaphore_signal(barrier, inc=1, device_id=left, device_id_type=MESH)
 
+    loads[0].wait()
+    loads[1].wait()
     ids = id_ref[...]
     ids_row = ids.astype(F32)
     ids_col = to_column(ids_row)
@@ -121,8 +125,8 @@
     gate_row = gate_ref[...].astype(F32).reshape(1, TOK)
     gate_col = to_column(gate_row)
 
-    loads[0].wait()
-    loads[1].wait()
+    loads[2].wait()
+    loads[3].wait()
     og[...] = (gate_col * og[...].astype(F32)).astype(BF)
 
     pl.semaphore_wait(barrier, 17 + (zl < NZ - 1).astype(jnp.int32) + (zl > 0).astype(jnp.int32))
@@ -152,7 +156,7 @@
                 dispatch(h, i).start()
     relay(0, 0).start()
     rows[0, 0, 0, 0] = slots[0, 0]
-    for load in loads[2:]:
+    for load in loads[4:]:
         load.wait()
 
     def rows_of(who, h, q):
@@ -498,9 +502,11 @@
             jax.ShapeDtypeStruct((64, FF), F32),
             jax.ShapeDtypeStruct((128, D), F32),
         ),
-        in_specs=[any_spec, any_spec, vmem, vmem, any_spec, any_spec],
+        in_specs=[any_spec] * 6,
         out_specs=(vmem, vmem, vmem, vmem),
         scratch_shapes=[
+            pltpu.VMEM((TOK,), BF),
+            pltpu.VMEM((1, TOK), jnp.int32),
             pltpu.VMEM((TOK, D), BF),
             pltpu.VMEM((TOK, D), BF),
             pltpu.VMEM((D, 1024), BF),
@@ -518,20 +524,20 @@
             pltpu.VMEM((64, 1024), F32),
             pltpu.VMEM((4, 2, 64, 1024), F32),
             pltpu.VMEM((4, 128, D), F32),
-            dma((6,)),
+            dma((8,)),
             dma((2, 8)), dma((2, 8)), dma((2, 8)), dma((2, 8)),
             dma((2, 2)), dma((2, 2)), dma((2, 2)), dma((2, 2)),
             dma((2, 8)), dma((2, 8)), dma((2, 8)), dma((2, 8)),
             dma((2, 4)), dma((2, 4)), dma((2, 4)), dma((2, 4)), dma((2, 4)), dma((1,)), dma((1,)),
         ],
         compiler_params=pltpu.CompilerParams(
-            collective_id=0, has_side_effects=True, vmem_limit_bytes=50 * 1024 * 1024
+            collective_id=0, has_side_effects=True, vmem_limit_bytes=52 * 1024 * 1024
         ),
     )(
-        tokens,
-        out_grad,
-        gate_prob,
-        expert_id.reshape(1, TOK),
+        *(
+            pltpu.with_memory_space_constraint(x, pltpu.HBM)
+            for x in (tokens, out_grad, gate_prob, expert_id.reshape(1, TOK))
+        ),
         up_weight[0],
         down_weight[0],
     )

time: 127 us -> 124 us (0.976)
  local copies, waits for them, and re-layouts: 3.41 us -> 0 us
    unnamed x8 -> x0, local copies, waits for them, and re-layouts: 3.41 us -> none
where the time goes in v6:
time: 124 us; the launch traced here: 121 us
  Pallas kernels  121 us (98%)
    pallas_call x1, Pallas kernels, per_device(): pl.pallas_call(kernel, out_shape=(jax.ShapeDtypeStruct((TOK, D), BF), jax...  119 us

profile of v6, /device:TPU:64, one launch (start us, length us, event | category | flops | bytes accessed | tf_op | source)
XLA Modules:
  0.0 121.5 jit_solution(6884244857197966343)
XLA Ops:
  0.6 119.2 %shard_map.93 = (bf16[256,1024]{1,0:T(8,128)(2,1)S(1)}, bf16[1,256]{1,0:T(2,128)(2,1)S(1)}, f32[64,2048]{1,0:T(8,128)S(1)}, f32[128,1024]{1,0:T(8,128)S(1)}) custom-call(bf16[256,1024]{1,0:T(8,128)(2,1)} %tok_hbm.1, bf16[256,1024]{1,0:T(8,128)(2,1)} %og_hbm.1, bf16[256]{0:T(256)(128)(2,1)} %gate_hbm.1, s32[1,256]{1,0:T(1,128)} %bitcast.7, ...), custom_call_target="tpu_custom_call" | custom-call | tf_op jit(solution)/shard_map/pallas_call | solution.py:497
  119.8 1.7 %shard_map.94 = (bf16[256,1024]{1,0:T(8,128)(2,1)}, bf16[256]{0:T(256)(128)(2,1)}, f32[64,2048]{1,0:T(8,128)}, f32[128,1024]{1,0:T(8,128)}) custom-call(bf16[256,1024]{1,0:T(8,128)(2,1)S(1)} %get-tuple-element.12.tg_in, bf16[1,256]{1,0:T(2,128)(2,1)S(1)} %get-tuple-element.13.gg_in, f32[64,2048]{1,0:T(8,128)S(1)} %get-tuple-element.14.ug_in, ...), custom_call_target="tpu_custom_call" | custom-call | tf_op jit(solution)/shard_map/pallas_call | solution.py:544

commit v7 on v4

--- a/solution.py
+++ b/solution.py
@@ -35,9 +35,9 @@
 
 
 def kernel(
-    tok_hbm, og_hbm, gate_ref, id_ref, upw_hbm, dnw_hbm,
+    tok_hbm, og_hbm, gate_hbm, id_hbm, upw_hbm, dnw_hbm,
     tg_ref, gg_ref, ug_ref, dg_ref,
-    tok, og, upw, dnw, slots, rows, hidden, pregrad, fgp, fgr, fgs, back,
+    gate_ref, id_ref, tok, og, upw, dnw, slots, rows, hidden, pregrad, fgp, fgr, fgs, back,
     gown, gp, gr, ggs, ggback,
     su_out, sd_out, su_in, sd_in, zu, zd, zlu, zld, zru, zrd, fu, fd, xu, pu, pd,
     in_sem, ds_sem, dr_sem, as_sem, ar_sem, fs_sem, fr_sem, hs_sem, hr_sem,
@@ -73,6 +73,8 @@
     pairs = [(h, i) for h in (1, 0) for i in range(8) if (h, i) != (0, 0)]
 
     sources = [
+        (id_hbm, id_ref),
+        (gate_hbm, gate_ref),
         (tok_hbm, tok),
         (og_hbm, og),
         (upw_hbm.at[:, pl.ds(pl.multiple_of(y * 512, 512), 512)], upw.at[:, 0:512]),
@@ -100,6 +102,8 @@
     def _():
         pl.semaphore_signal(barrier, inc=1, device_id=left, device_id_type=MESH)
 
+    loads[0].wait()
+    loads[1].wait()
     ids = id_ref[...]
     ids_row = ids.astype(F32)
     ids_col = to_column(ids_row)
@@ -120,11 +124,11 @@
 
     slot_row = slot_of(ids_row, pos_row)
     slot_col = slot_of(ids_col, pos_col)
-    gate_row = gate_ref[...].astype(F32)
+    gate_row = gate_ref[...].astype(F32).reshape(1, TOK)
     gate_col = to_column(gate_row)
 
-    loads[0].wait()
-    loads[1].wait()
+    loads[2].wait()
+    loads[3].wait()
     og[...] = (gate_col * og[...].astype(F32)).astype(BF)
 
     pl.semaphore_wait(barrier, 17 + (zl < NZ - 1).astype(jnp.int32) + (zl > 0).astype(jnp.int32))
@@ -154,7 +158,7 @@
                 dispatch(h, i).start()
     relay(0, 0).start()
     rows[0, 0, 0, 0] = slots[0, 0]
-    for load in loads[2:]:
+    for load in loads[4:]:
         load.wait()
 
     def forward(h, first, count):
@@ -260,8 +264,7 @@
             for i in range(first, first + count):
                 relay(h, i).wait_recv()
             forward(h, first, count)
-        if not final:
-            mate_part(h, q)
+        mate_part(h, q)
         last = (h, q)
 
     low = 1 - zl // 2
@@ -376,38 +379,34 @@
 
     edge = (zl == 0) | (zl == NZ - 1)
 
-    down_part(1, 0, emit_down_out)
-    for n in range(2):
-        ysend(1, block(n)).start()
-    down_part(0, 0, emit_down_own)
-    mate_part(1, 1)
-
-    @pl.when(edge)
-    def _():
-        step(1, 0)
-
     up_part(yf, yd, emit_up_out)
     for n in range(4):
         ysend(0, block(n)).start()
+    up_part(y, yr, emit_up_own)
+
+    @pl.when(edge)
+    def _():
+        step(0, 0)
+
     finish(*last)
-    up_part(y, yr, emit_up_own)
+    for pair in (0, 2):
+        down_part(1, pair, emit_down_out)
+        for n in range(pair, pair + 2):
+            ysend(1, block(n)).start()
 
     @pl.when(jnp.logical_not(edge))
     def _():
-        step(1, 0)
-
-    step(1, 1)
-    step(0, 0)
-    down_part(1, 2, emit_down_out)
-    for n in range(2, 4):
-        ysend(1, block(n)).start()
+        step(0, 0)
+
+    down_part(0, 0, emit_down_own)
     down_part(0, 2, emit_down_own)
 
     @pl.loop(1, 4)
     def _(n):
         step(0, n)
 
-    step(1, 2)
+    for n in range(2):
+        step(1, n)
 
     def settle(t, final):
         _, from_left, from_right = zrefs[t]
@@ -429,7 +428,8 @@
         device_id=mate, device_id_type=MESH,
     )
     swap.start()
-    step(1, 3)
+    for n in range(2, 4):
+        step(1, n)
 
     for h, i in pairs:
         give_back(h, i).wait_recv()
@@ -488,18 +488,14 @@
             zright(1, k).wait_send()
 
 
-def tail(tg_in, gg_in, ug_in, dg_in, tg_out, gg_out, ug_out, dg_out, tg, ug, dg, sem_in, sem_out):
-    moves = ((tg_in, tg, tg_out), (ug_in, ug, ug_out), (dg_in, dg, dg_out))
-    ins = [pltpu.make_async_copy(a, b, sem_in.at[n]) for n, (a, b, _) in enumerate(moves)]
-    outs = [pltpu.make_async_copy(b, c, sem_out.at[n]) for n, (_, b, c) in enumerate(moves)]
-    for copy in ins:
+def tail(tg_in, gg_in, ug_in, dg_in, tg_out, gg_out, ug_out, dg_out, sem):
+    moves = ((tg_in, tg_out), (ug_in, ug_out), (dg_in, dg_out))
+    copies = [pltpu.make_async_copy(a, b, sem.at[n]) for n, (a, b) in enumerate(moves)]
+    for copy in copies:
         copy.start()
-    gg_out[...] = gg_in[...]
-    for arrive, leave in zip(ins, outs):
-        arrive.wait()
-        leave.start()
-    for leave in outs:
-        leave.wait()
+    gg_out[...] = gg_in[...].reshape(TOK)
+    for copy in copies:
+        copy.wait()
 
 
 def per_device(tokens, out_grad, gate_prob, expert_id, up_weight, down_weight):
@@ -518,9 +514,11 @@
             jax.ShapeDtypeStruct((64, FF), F32),
             jax.ShapeDtypeStruct((128, D), F32),
         ),
-        in_specs=[any_spec, any_spec, vmem, vmem, any_spec, any_spec],
+        in_specs=[any_spec] * 6,
         out_specs=(vmem, vmem, vmem, vmem),
         scratch_shapes=[
+            pltpu.VMEM((TOK,), BF),
+            pltpu.VMEM((1, TOK), jnp.int32),
             pltpu.VMEM((TOK, D), BF),
             pltpu.VMEM((TOK, D), BF),
             pltpu.VMEM((D, 1024), BF),
@@ -538,20 +536,20 @@
             pltpu.VMEM((64, 1024), F32),
             pltpu.VMEM((4, 2, 64, 1024), F32),
             pltpu.VMEM((4, 128, D), F32),
-            dma((6,)),
+            dma((8,)),
             dma((2, 8)), dma((2, 8)), dma((2, 8)), dma((2, 8)),
             dma((2, 2)), dma((2, 2)), dma((2, 2)), dma((2, 2)),
             dma((2, 8)), dma((2, 8)), dma((2, 8)), dma((2, 8)),
             dma((2, 4)), dma((2, 4)), dma((2, 4)), dma((2, 4)), dma((2, 4)), dma((1,)), dma((1,)),
         ],
         compiler_params=pltpu.CompilerParams(
-            collective_id=0, has_side_effects=True, vmem_limit_bytes=60 * 1024 * 1024
+            collective_id=0, has_side_effects=True, vmem_limit_bytes=52 * 1024 * 1024
         ),
     )(
-        tokens,
-        out_grad,
-        gate_prob.reshape(1, TOK),
-        expert_id.reshape(1, TOK),
+        *(
+            pltpu.with_memory_space_constraint(x, pltpu.HBM)
+            for x in (tokens, out_grad, gate_prob, expert_id.reshape(1, TOK))
+        ),
         up_weight[0],
         down_weight[0],
     )
@@ -559,21 +557,18 @@
         tail,
         out_shape=(
             jax.ShapeDtypeStruct((TOK, D), BF),
-            jax.ShapeDtypeStruct((1, TOK), BF),
+            jax.ShapeDtypeStruct((TOK,), BF),
             jax.ShapeDtypeStruct((64, FF), F32),
             jax.ShapeDtypeStruct((128, D), F32),
         ),
-        in_specs=[any_spec, vmem, any_spec, any_spec],
+        in_specs=[vmem, vmem, vmem, vmem],
         out_specs=(any_spec, vmem, any_spec, any_spec),
         scratch_shapes=[
-            pltpu.VMEM((TOK, D), BF),
-            pltpu.VMEM((64, FF), F32),
-            pltpu.VMEM((128, D), F32),
-            dma((3,)),
             dma((3,)),
         ],
+        compiler_params=pltpu.CompilerParams(vmem_limit_bytes=2 * 1024 * 1024),
     )(tg, gg, ug, dg)
-    return tg, gg.reshape(TOK), ug[None], dg[None]
+    return tg, gg, ug[None], dg[None]
 
 
 def solution(mesh):

time: 130 us -> 125 us (0.962)
  Pallas kernels: 126 us -> 122 us
    pallas_call x1, Pallas kernels: 122 us -> 120 us  [per_device(): pl.pallas_call(kernel, out_shape=(jax.ShapeDtypeStruct((TOK, D), BF), jax...]
    pallas_call x1, Pallas kernels: 3.47 us -> 1.68 us  [per_device(): pl.pallas_call(tail, out_shape=(jax.ShapeDtypeStruct((TOK, D), BF), jax.S...]
where the time goes in v7:
time: 125 us; the launch traced here: 123 us
  Pallas kernels  122 us (98%)
    pallas_call x1, Pallas kernels, per_device(): pl.pallas_call(kernel, out_shape=(jax.ShapeDtypeStruct((TOK, D), BF), jax...  120 us

profile of v7, /device:TPU:64, one launch (start us, length us, event | category | flops | bytes accessed | tf_op | source)
XLA Modules:
  0.0 122.6 jit_solution(3094585946946182911)
XLA Ops:
  0.6 120.1 %shard_map.93 = (bf16[256,1024]{1,0:T(8,128)(2,1)S(1)}, bf16[1,256]{1,0:T(2,128)(2,1)S(1)}, f32[64,2048]{1,0:T(8,128)S(1)}, f32[128,1024]{1,0:T(8,128)S(1)}) custom-call(bf16[256,1024]{1,0:T(8,128)(2,1)} %tok_hbm.1, bf16[256,1024]{1,0:T(8,128)(2,1)} %og_hbm.1, bf16[256]{0:T(256)(128)(2,1)} %gate_hbm.1, s32[1,256]{1,0:T(1,128)} %bitcast.7, ...), custom_call_target="tpu_custom_call" | custom-call | tf_op jit(solution)/shard_map/pallas_call | solution.py:509
  120.7 1.7 %shard_map.94 = (bf16[256,1024]{1,0:T(8,128)(2,1)}, bf16[256]{0:T(256)(128)(2,1)}, f32[64,2048]{1,0:T(8,128)}, f32[128,1024]{1,0:T(8,128)}) custom-call(bf16[256,1024]{1,0:T(8,128)(2,1)S(1)} %get-tuple-element.12.tg_in, bf16[1,256]{1,0:T(2,128)(2,1)S(1)} %get-tuple-element.13.gg_in, f32[64,2048]{1,0:T(8,128)S(1)} %get-tuple-element.14.ug_in, ...), custom_call_target="tpu_custom_call" | custom-call | tf_op jit(solution)/shard_map/pallas_call | solution.py:556
